TPU v7x, 128 devices: a whole 4x4x4 slice. The times are simulated.
128 devices in a mesh: band: 8 (over y_hi, z), fft: 16 (over y_lo, x, core).
Axes of the slice: x: 4, y: 4 (y_hi: 2, y_lo: 2; y = y_hi * 2 + y_lo), z: 4, core: 2. Of those that a mesh axis runs over, the one named last changes fastest.
Arguments:
- band_coeffs: float32 [16, 1024, 192], P('band', 'fft'), may hold values from -6 to 6
- potential: float32 [192, 192, 192], P('fft'), may hold values from -12 to 12
- stick_column: int32 [1024], replicated, may hold values from 0 to 9215, as said below
- stick_length: int32 [1024], P('fft'), may hold values from 1 to 96
- orbitals: bfloat16 [512, 1024, 192], P(None, ('band', 'fft')), may hold values from -0.078125 to 0.078125
Outputs:
- applied: bfloat16 [16, 1024, 192], P('band', 'fft')
- margin: float32 [512, 32], P(('band', 'fft'))
Inputs may be any that keep to these rules, and one draw needn't show every extreme that they name: `stick_column`: distinct columns of a 96 x 96 frequency box; column q stands for gx = q // 96 - 96/2 and gy = q % 96 - 96/2.
All inputs are finite; a program needn't handle non-finite values.
Results may differ from a plain program's by a relative error of at most 0.0055.
Values may be sent and summed in bfloat16 or wider, within the bound.
A program may use at most 64 MiB of HBM per device.

v0:
```python
import math

import jax
import jax.numpy as jnp
from jax import lax
from jax.sharding import PartitionSpec as P

HIGHEST_MODE = lax.Precision.HIGHEST


def phase_tables(half_box, grid_cells):
    frequency = jnp.arange(half_box, dtype=jnp.int32) - half_box // 2
    positions = jnp.arange(grid_cells, dtype=jnp.int32)
    turn_count = frequency[:, None] * positions[None, :] % grid_cells
    angles = turn_count.astype(jnp.float32) * (2.0 * math.pi / grid_cells)
    cosine = jnp.cos(angles)
    sine_part = jnp.sin(angles)
    forward = jnp.stack([jnp.stack([cosine, sine_part], 1), jnp.stack([-sine_part, cosine], 1)], 0)
    cos_back = cosine.T
    sin_back = sine_part.T
    backward = jnp.stack(
        [jnp.stack([cos_back, -sin_back], 1), jnp.stack([sin_back, cos_back], 1)], 0
    )
    return (forward, backward)


def per_device(band_coeffs, potential, stick_column, stick_length, orbitals):
    band_dev, sticks_dev, coef_width = band_coeffs.shape
    half_box = coef_width // 2
    grid_cells = potential.shape[1]
    forward, backward = phase_tables(half_box, grid_cells)
    first_stick = lax.axis_index("fft") * sticks_dev
    own_columns = lax.dynamic_slice_in_dim(stick_column, first_stick, sticks_dev)
    z_freq = jnp.arange(half_box, dtype=jnp.int32) - half_box // 2
    stick_len = stick_length[:, None]
    live_slots = (z_freq[None, :] >= -(stick_len // 2)) & (
        z_freq[None, :] < stick_len - stick_len // 2
    )
    x_freq = own_columns // half_box - half_box // 2
    y_freq = own_columns % half_box - half_box // 2
    kinetic = (x_freq[:, None] ** 2 + y_freq[:, None] ** 2 + z_freq[None, :] ** 2).astype(
        jnp.float32
    ) * (2.0 / (half_box * half_box))
    norm_factor = 1.0 / float(grid_cells) ** 3
    live_mask = live_slots[:, None, :]
    kinetic_mask = kinetic[:, None, :]
    box_index = jnp.arange(half_box, dtype=jnp.int32)
    onehot_x = (box_index[:, None] == (stick_column // half_box)[None, :]).astype(jnp.float32)
    onehot_y = ((stick_column % half_box)[:, None] == box_index[None, :]).astype(jnp.float32)

    def place_plane(plane_vals):
        spread = plane_vals[..., None] * onehot_y
        return jnp.einsum("xs,bcsy->bcxy", onehot_x, spread, precision=HIGHEST_MODE)

    def pick_plane(plane_box):
        rows_x = jnp.einsum("xs,bcxy->bcsy", onehot_x, plane_box, precision=HIGHEST_MODE)
        return jnp.sum(rows_x * onehot_y, axis=-1)

    def apply_hamiltonian(coeffs_in):
        band_count = coeffs_in.shape[0]
        masked = jnp.where(live_mask, coeffs_in.reshape(band_count, sticks_dev, 2, half_box), 0.0)
        columns = jnp.einsum("bsck,ckdz->bdzs", masked, forward, precision=HIGHEST_MODE)
        planes = lax.all_to_all(
            columns.astype(jnp.bfloat16), "fft", split_axis=2, concat_axis=3, tiled=True
        ).astype(columns.dtype)
        freq_box = lax.map(place_plane, jnp.moveaxis(planes, 2, 0))
        freq_box = jnp.moveaxis(freq_box, 0, 2)
        half_done = jnp.einsum("bcpxk,ckdy->bdpxy", freq_box, forward, precision=HIGHEST_MODE)
        real_field = jnp.einsum("bcpky,ckdx->bdpxy", half_done, forward, precision=HIGHEST_MODE)
        real_field = real_field * potential[None, None]
        half_done = jnp.einsum("bcpxy,cxdk->bdpky", real_field, backward, precision=HIGHEST_MODE)
        freq_box = jnp.einsum("bcpky,cydq->bdpkq", half_done, backward, precision=HIGHEST_MODE)
        picked = lax.map(pick_plane, jnp.moveaxis(freq_box, 2, 0))
        picked = jnp.moveaxis(picked, 0, 2)
        stick_data = lax.all_to_all(
            picked.astype(jnp.bfloat16), "fft", split_axis=3, concat_axis=2, tiled=True
        ).astype(picked.dtype)
        local_term = (
            jnp.einsum("bczs,czdk->bsdk", stick_data, backward, precision=HIGHEST_MODE)
            * norm_factor
        )
        h_coeffs = jnp.where(live_mask, kinetic_mask * masked + local_term, 0.0)
        return h_coeffs.astype(jnp.bfloat16).reshape(band_count, sticks_dev, coef_width)

    applied = jnp.concatenate(
        [
            apply_hamiltonian(band_coeffs[band_index : band_index + 1])
            for band_index in range(band_dev)
        ],
        0,
    )
    gathered = lax.all_to_all(applied, "band", split_axis=1, concat_axis=0, tiled=True)
    real_part = gathered[:, :, :half_box]
    imag_part = gathered[:, :, half_box:]
    stacked = jnp.concatenate([gathered, jnp.concatenate([imag_part, -real_part], 2)], 0)
    stacked = stacked.reshape(stacked.shape[0], -1)
    orbital_rows = orbitals.reshape(orbitals.shape[0], -1)
    margin = lax.psum_scatter(
        lax.dot_general(
            orbital_rows, stacked, (((1,), (1,)), ((), ())), preferred_element_type=jnp.float32
        ),
        ("band", "fft"),
        scatter_dimension=0,
        tiled=True,
    )
    return (applied, margin)


def solution(mesh):
    placed = (
        P("band", "fft", None),
        P("fft", None, None),
        P(),
        P("fft"),
        P(None, ("band", "fft"), None),
    )
    return jax.shard_map(
        per_device,
        mesh=mesh,
        in_specs=placed,
        out_specs=(P("band", "fft", None), P(("band", "fft"), None)),
        check_vma=False,
    )
```

profile of v0, /device:TPU:1, one launch (start us, length us, event | category | flops | bytes accessed | tf_op | source)
XLA Modules:
  0.0 321.2 jit_solution(7054145985036065035)
XLA Ops:
  11.4 6.8 %all-to-all-start.2 = ((bf16[16,2,768]{2,1,0:T(2,128)(2,1)}), bf16[16,2,768]{2,1,0:T(2,128)(2,1)S(1)}, u32[]{:S(2)}, u32[]{:S(2)}) async-start(bf16[16,2,768]{2,1,0:T(2,128)(2,1)} %reshape.499), calls=%async_computation.2 | async-start | bytes 98304 | tf_op jit(solution)/shard_map/all_to_all | solution.py:63
  20.9 3.1 all-to-all-done.2
  24.0 4.3 %all-to-all-start = ((bf16[16,2,768]{2,1,0:T(2,128)(2,1)}), bf16[16,2,768]{2,1,0:T(2,128)(2,1)}, u32[]{:S(2)}, u32[]{:S(2)}) async-start(bf16[16,2,768]{2,1,0:T(2,128)(2,1)} %reshape.495), calls=%async_computation | async-start | bytes 98304 | tf_op jit(solution)/shard_map/all_to_all | solution.py:63
  29.4 18.8 %while.46 = (s32[]{:T(128)}, f32[12,1,2,96,96]{3,4,2,1,0:T(8,128)S(1)}, f32[12,1,2,1024]{3,2,1,0:T(2,128)}, s32[1024]{0:T(1024)S(1)}, s32[1024]{0:T(1024)S(1)}, /*index=5*/s32[]{:T(128)}) while((s32[]{:T(128)}, f32[12,1,2,96,96]{3,4,2,1,0:T(8,128)S(1)}, f32[12,1,2,1024]{3,2,1,0:T(2,128)}, s32[1024]{0:T(1024)S(1)}, ...), condition=%wide.region_6.7_spmd.clone, body=%wide.region_5.6_spmd.clone.sunk | while | flops 227082240 | bytes 917581 | solution.py:66
  48.3 2.1 fusion.84
  50.4 9.3 %fusion.50 = f32[2,12,192,192]{3,2,1,0:T(8,128)S(1)} fusion(f32[12,192,192]{2,1,0:T(8,128)S(1)} %copy-done.1, f32[2,192,12,96,1]{3,1,4,2,0:T(8,128)S(1)} %fusion.84, f32[1,96,2,192]{3,1,0,2:T(8,128)S(1)} %get-tuple-element.333, f32[1,96,2,192]{3,1,0,2:T(8,128)S(1)} %get-tuple-element.332), kind=kOutput, calls=%fused_computation.59 | convolution fusion | flops 2039390208 | bytes 7372800 | tf_op jit(solution)/shard_map/bcpky,ckdx->bdpxy/dot_general | solution.py:69
  59.7 4.4 %fusion.75 = f32[2,12,96,192]{3,2,1,0:T(8,128)S(1)} fusion(f32[2,12,192,192]{3,2,1,0:T(8,128)S(1)} %fusion.50, f32[1,192,2,96]{1,3,0,2:T(8,128)S(1)} %get-tuple-element.331, f32[1,192,2,96]{1,3,0,2:T(8,128)S(1)} %get-tuple-element.330), kind=kOutput, calls=%fused_computation.79 | convolution fusion | flops 2038505472 | bytes 5603328 | tf_op jit(solution)/shard_map/bcpxy,cxdk->bdpky/dot_general | solution.py:71
  64.1 2.7 fusion.81
  67.5 17.7 %while.47 = (s32[]{:T(128)}, bf16[12,1,2,1024]{3,2,1,0:T(2,128)(2,1)}, f32[12,1,2,96,96]{3,4,0,2,1:T(8,128)S(1)}, s32[1024]{0:T(1024)S(1)}, s32[1024]{0:T(1024)S(1)}, /*index=5*/s32[]{:T(128)}) while((s32[]{:T(128)}, bf16[12,1,2,1024]{3,2,1,0:T(2,128)(2,1)}, f32[12,1,2,96,96]{3,4,0,2,1:T(8,128)S(1)}, s32[1024]{0:T(1024)S(1)}, ...), condition=%wide.region_9.10_spmd.clone, body=%wide.region_7.9_spmd.clone.sunk | while | flops 227276800 | bytes 905801 | solution.py:73
  86.7 1.5 reshape.501
  88.3 5.8 %all-to-all-start.3 = ((bf16[16,2,768]{2,1,0:T(2,128)(2,1)}), bf16[16,2,768]{2,1,0:T(2,128)(2,1)}, u32[]{:S(2)}, u32[]{:S(2)}) async-start(bf16[16,2,768]{2,1,0:T(2,128)(2,1)} %reshape.501), calls=%async_computation.3 | async-start | bytes 98304 | tf_op jit(solution)/shard_map/all_to_all | solution.py:75
  96.0 19.1 %while.44 = (s32[]{:T(128)}, f32[12,1,2,96,96]{3,4,2,1,0:T(8,128)S(1)}, f32[12,1,2,1024]{3,2,1,0:T(2,128)}, s32[1024]{0:T(1024)S(1)}, s32[1024]{0:T(1024)S(1)}, /*index=5*/s32[]{:T(128)}) while((s32[]{:T(128)}, f32[12,1,2,96,96]{3,4,2,1,0:T(8,128)S(1)}, f32[12,1,2,1024]{3,2,1,0:T(2,128)}, s32[1024]{0:T(1024)S(1)}, ...), condition=%wide.region_1.2_spmd.clone, body=%wide.region_0.1_spmd.clone.sunk | while | flops 227082240 | bytes 917581 | solution.py:66
  115.1 2.1 fusion.86
  117.2 9.3 %fusion.51 = f32[2,12,192,192]{3,2,1,0:T(8,128)S(1)} fusion(f32[12,192,192]{2,1,0:T(8,128)S(1)} %copy-done.2, f32[2,192,12,96,1]{3,1,4,2,0:T(8,128)S(1)} %fusion.86, f32[1,96,2,192]{3,1,0,2:T(8,128)S(1)} %get-tuple-element.333, f32[1,96,2,192]{3,1,0,2:T(8,128)S(1)} %get-tuple-element.332), kind=kOutput, calls=%fused_computation.61 | convolution fusion | flops 2039390208 | bytes 7372800 | tf_op jit(solution)/shard_map/bcpky,ckdx->bdpxy/dot_general | solution.py:69
  126.5 4.4 %fusion.72 = f32[2,12,96,192]{3,2,1,0:T(8,128)S(1)} fusion(f32[2,12,192,192]{3,2,1,0:T(8,128)S(1)} %fusion.51, f32[1,192,2,96]{1,3,0,2:T(8,128)S(1)} %get-tuple-element.331, f32[1,192,2,96]{1,3,0,2:T(8,128)S(1)} %get-tuple-element.330), kind=kOutput, calls=%fused_computation.78 | convolution fusion | flops 2038505472 | bytes 5603328 | tf_op jit(solution)/shard_map/bcpxy,cxdk->bdpky/dot_general | solution.py:71
  130.9 2.7 fusion.78
  133.6 10.9 %while.45 = (s32[]{:T(128)}, bf16[12,1,2,1024]{3,2,1,0:T(2,128)(2,1)S(1)}, f32[12,1,2,96,96]{3,4,0,2,1:T(8,128)S(1)}, s32[1024]{0:T(1024)S(1)}, s32[1024]{0:T(1024)S(1)}, /*index=5*/s32[]{:T(128)}) while((s32[]{:T(128)}, bf16[12,1,2,1024]{3,2,1,0:T(2,128)(2,1)S(1)}, f32[12,1,2,96,96]{3,4,0,2,1:T(8,128)S(1)}, s32[1024]{0:T(1024)S(1)}, ...), condition=%wide.region_4.5_spmd.clone, body=%wide.region_2.4_spmd.clone.sunk | while | flops 227276800 | bytes 905293 | solution.py:73
  145.4 1.6 reshape.497
  147.0 5.8 %all-to-all-start.1 = ((bf16[16,2,768]{2,1,0:T(2,128)(2,1)}), bf16[16,2,768]{2,1,0:T(2,128)(2,1)S(1)}, u32[]{:S(2)}, u32[]{:S(2)}) async-start(bf16[16,2,768]{2,1,0:T(2,128)(2,1)} %reshape.497), calls=%async_computation.1 | async-start | bytes 98304 | tf_op jit(solution)/shard_map/all_to_all | solution.py:75
  152.8 2.0 reshape.502
  156.1 2.5 all-to-all-done.1
  158.6 1.2 reshape.498
  161.1 13.9 %all_to_all.66 = bf16[2,64,192]{2,0,1:T(2,128)(2,1)S(1)} all-to-all(bf16[2,64,192]{2,0,1:T(2,128)(2,1)S(1)} %copy.207), channel_id=1, replica_groups=mesh['band'=8,'fft'=16] {'band'}, dimensions={1} | all-to-all | bytes 98304 | tf_op jit(solution)/shard_map/all_to_all | solution.py:92
  176.3 136.4 %all-reduce.3.cloned.1.call-done = f32[512,32]{0,1:T(8,128)} async-done(((f32[512,32]{0,1:T(8,128)}), f32[512,32]{0,1:T(8,128)}) %all-reduce.3.cloned.1.call-update) | async-done | bytes 65552
  (226 shorter events, 82.9 us)
Async XLA Ops:
  7.2 168.1 %copy-start = (bf16[512,8,192]{0,2,1:T(8,128)(2,1)S(1)}, bf16[512,8,192]{0,2,1:T(8,128)(2,1)}, u32[]{:S(2)}) copy-start(bf16[512,8,192]{0,2,1:T(8,128)(2,1)} %param.17) | copy-start | bytes 4718596
  7.2 11.5 %copy-start.9 = (s32[1024]{0:T(1024)S(1)}, s32[1024]{0:T(1024)}, u32[]{:S(2)}) copy-start(s32[1024]{0:T(1024)} %param.15) | copy-start | bytes 12292
  10.0 10.0 %copy-start.3 = (f32[64,2,96]{2,1,0:T(2,128)}, f32[64,2,96]{2,1,0:T(2,128)S(1)}, u32[]{:S(2)}) copy-start(f32[64,2,96]{2,1,0:T(2,128)S(1)} %reshape.446) | copy-start | bytes 147460
  11.4 12.6 %all-to-all-start.2 = ((bf16[16,2,768]{2,1,0:T(2,128)(2,1)}), bf16[16,2,768]{2,1,0:T(2,128)(2,1)S(1)}, u32[]{:S(2)}, u32[]{:S(2)}) async-start(bf16[16,2,768]{2,1,0:T(2,128)(2,1)} %reshape.499), calls=%async_computation.2 | async-start | bytes 98304 | tf_op jit(solution)/shard_map/all_to_all | solution.py:63
  19.0 1.1 copy-start.5
  24.0 64.2 %all-to-all-start = ((bf16[16,2,768]{2,1,0:T(2,128)(2,1)}), bf16[16,2,768]{2,1,0:T(2,128)(2,1)}, u32[]{:S(2)}, u32[]{:S(2)}) async-start(bf16[16,2,768]{2,1,0:T(2,128)(2,1)} %reshape.495), calls=%async_computation | async-start | bytes 98304 | tf_op jit(solution)/shard_map/all_to_all | solution.py:63
  48.3 2.1 copy-start.1
  88.3 58.7 %all-to-all-start.3 = ((bf16[16,2,768]{2,1,0:T(2,128)(2,1)}), bf16[16,2,768]{2,1,0:T(2,128)(2,1)}, u32[]{:S(2)}, u32[]{:S(2)}) async-start(bf16[16,2,768]{2,1,0:T(2,128)(2,1)} %reshape.501), calls=%async_computation.3 | async-start | bytes 98304 | tf_op jit(solution)/shard_map/all_to_all | solution.py:75
  115.1 2.1 copy-start.2
  144.6 11.0 %copy-start.4 = (f32[64,2,96]{2,1,0:T(2,128)S(1)}, f32[64,2,96]{2,1,0:T(2,128)}, u32[]{:S(2)}) copy-start(f32[64,2,96]{2,1,0:T(2,128)} %copy-done.3) | copy-start | bytes 147460
  144.6 11.0 %copy-start.7 = (f32[64,96]{1,0:T(8,128)S(1)}, f32[64,96]{1,0:T(8,128)}, u32[]{:S(2)}) copy-start(f32[64,96]{1,0:T(8,128)} %convert_multiply_fusion) | copy-start | bytes 73732
  145.4 15.1 %copy-start.6 = (f32[64,2,96]{2,1,0:T(2,128)S(1)}, f32[64,2,96]{2,1,0:T(2,128)}, u32[]{:S(2)}) copy-start(f32[64,2,96]{2,1,0:T(2,128)} %copy-done.5) | copy-start | bytes 147460
  147.0 11.6 %all-to-all-start.1 = ((bf16[16,2,768]{2,1,0:T(2,128)(2,1)}), bf16[16,2,768]{2,1,0:T(2,128)(2,1)S(1)}, u32[]{:S(2)}, u32[]{:S(2)}) async-start(bf16[16,2,768]{2,1,0:T(2,128)(2,1)} %reshape.497), calls=%async_computation.1 | async-start | bytes 98304 | tf_op jit(solution)/shard_map/all_to_all | solution.py:75
  152.8 159.9 %all-reduce.3.cloned.1.call-start = ((), (), s32[]{:S(2)}) async-start(), calls=%async_computation.5 | async-start | bytes 131072
  161.1 153.1 %copy-start.8 = (bf16[2,64,192]{2,1,0:T(8,128)(2,1)}, bf16[2,64,192]{2,1,0:T(8,128)(2,1)S(1)}, u32[]{:S(2)}) copy-start(bf16[2,64,192]{2,1,0:T(8,128)(2,1)S(1)} %constant_dynamic-update-slice_fusion) | copy-start | bytes 147460
Sparse Core Ops, SparseCore 0:
  176.4 136.2 all-reduce.2
where the time goes:
time: 326 us; the launch traced here: 321 us
  waiting for transfers between devices  142 us (44%)
  matrix products  78.6 us (24%)
  local copies, waits for them, and re-layouts  42.6 us (13%)
  starting transfers between devices  22.7 us (7%)
  between operations  14.8 us (5%)
  blocking collectives  13.9 us (4%)
  other arithmetic  4.97 us (2%)
    unnamed x2, waiting for transfers between devices  136 us
    dot_general x24, matrix products, pick_plane(): jnp.einsum('xs,bcxy->bcsy', onehot_x, plane_box, precision=HIGHEST_MODE)  20 us
    dot_general x24, matrix products, place_plane(): return jnp.einsum('xs,bcsy->bcxy', onehot_x, spread, precision=HIGHEST_MODE)  19 us
    dot_general x2, matrix products, apply_hamiltonian(): jnp.einsum('bcpky,ckdx->bdpxy', half_done, forward, precision=HIGHEST_MODE)  18.5 us
    mul x24, local copies, waits for them, and re-layouts, place_plane(): spread = plane_vals[..., None] * onehot_y  16.8 us
    all_to_all x1, blocking collectives, per_device(): lax.all_to_all(applied, 'band', split_axis=1, concat_axis=0, tiled=True)  13.9 us
    all_to_all x2, starting transfers between devices, apply_hamiltonian(): lax.all_to_all(picked.astype(jnp.bfloat16), 'fft', split_axis=3, concat_a...  11.6 us
    unnamed x33, local copies, waits for them, and re-layouts  11.1 us
  transfers between devices with their start and end apart: 5, of which 3 were waited for; matrix products, arithmetic and copies ran while one was open for 36% of the time, Pallas kernels for 0%

commit v1 on v0

v1 whole, which is shorter than its diff:
```python
import functools
import math

import jax
import jax.numpy as jnp
import numpy as np
from jax import lax
from jax.experimental import pallas as pl
from jax.experimental.pallas import tpu as pltpu
from jax.sharding import PartitionSpec as P

BF = jnp.bfloat16
F32 = jnp.float32
MESH = pl.DeviceIdType.MESH
HIGH = lax.Precision.HIGHEST
VM = pl.BlockSpec(memory_space=pltpu.VMEM)


def dft_tables(half, grid):
    pad_to = -(-half // 128) * 128
    freq = np.arange(half) - half // 2
    angle = (freq[:, None] * np.arange(grid)[None, :] % grid) * (2.0 * math.pi / grid)
    co, si = np.cos(angle), np.sin(angle)
    pad = ((0, pad_to - half), (0, 0))
    cp, sp = np.pad(co, pad), np.pad(si, pad)
    fy = np.stack([np.concatenate([cp, -sp], 0), np.concatenate([sp, cp], 0)])
    fx = np.concatenate([np.concatenate([co.T, -si.T], 1), np.concatenate([si.T, co.T], 1)], 0)
    fxb = np.concatenate([np.concatenate([co, si], 1), np.concatenate([-si, co], 1)], 0)
    fyb = np.stack([np.concatenate([cp.T, -sp.T], 1), np.concatenate([sp.T, cp.T], 1)])
    fz = np.stack(
        [np.concatenate([co.T, -si.T], 1), np.concatenate([si.T, co.T], 1)], 1
    ).reshape(2 * grid, 2 * half)
    fzb = np.concatenate(
        [np.stack([co, si], -1).reshape(half, -1), np.stack([-si, co], -1).reshape(half, -1)], 0
    ) / float(grid) ** 3
    return fy, fx, fxb, fyb, fz, fzb


def greet(groups):
    barrier = pltpu.get_barrier_semaphore()
    total = 0
    for axis, n in groups:
        me = lax.axis_index(axis)
        for k in range(1, n):
            pl.semaphore_signal(
                barrier, inc=1, device_id={axis: lax.rem(me + k, n)}, device_id_type=MESH
            )
        total += n - 1
    pl.semaphore_wait(barrier, total)


def exchange(axis, n, src, dst, send_sem, recv_sem):
    me = lax.axis_index(axis)
    copies = []
    for k in range(1, n):
        peer = lax.rem(me + k, n)
        copies.append(
            pltpu.make_async_remote_copy(
                src_ref=src.at[peer],
                dst_ref=dst.at[me],
                send_sem=send_sem.at[k],
                recv_sem=recv_sem.at[k],
                device_id={axis: peer},
                device_id_type=MESH,
            )
        )
        copies[-1].start()
    own = pltpu.make_async_copy(src.at[me], dst.at[me], send_sem.at[0])
    own.start()
    own.wait()
    for copy in copies:
        copy.wait()


def live_of(length, half, lanes_of):
    lane = lax.broadcasted_iota(jnp.int32, lanes_of, 1)
    z_freq = lane % half - half // 2
    return (z_freq >= -(length // 2)) & (z_freq < length - length // 2), z_freq


def columns_kernel(n, coef, length, fz, out, send, send_sem, recv_sem):
    half = coef.shape[1] // 2
    live, _ = live_of(length[...], half, coef.shape)
    masked = jnp.where(live, coef[...], 0.0)
    cols = lax.dot_general(
        fz[...], masked, (((1,), (1,)), ((), ())), precision=HIGH, preferred_element_type=F32
    )
    send[...] = cols.reshape(send.shape).astype(BF)
    greet([("fft", n)])
    exchange("fft", n, send, out, send_sem, recv_sem)


def planes_kernel(half, recv, pot, col, fy, fx, fxb, fyb, out, ox, oxf, wyt, wy, cf, acc):
    nf, rows, lanes = recv.shape
    planes = pot.shape[0]
    sd = lanes // 2
    lane_pad = fy.shape[1] // 2
    for f in range(nf):
        c = col[f : f + 1, :]
        c = jnp.concatenate([c, c], axis=1)
        xs = c // half
        ys = c - xs * half
        sl = slice(f * lanes, (f + 1) * lanes)
        one = (lax.broadcasted_iota(jnp.int32, (half, lanes), 0) == xs).astype(F32)
        oxf[:, sl] = one
        ox[:, sl] = one.astype(BF)
        r = lax.broadcasted_iota(jnp.int32, (2 * lane_pad, lanes), 0)
        b = lax.broadcasted_iota(jnp.int32, (2 * lane_pad, lanes), 1) // sd
        w = (r == ys + b * lane_pad).astype(F32)
        wyt[:, sl] = w.astype(BF)
        wy[sl, :] = w.T.astype(BF)
        cf[f] = recv[f].astype(F32)

    def step(p, carry):
        parts = []
        for c in range(2):
            pieces = []
            for f in range(nf):
                row = cf[f, pl.ds(2 * p + c, 1), :]
                sl = slice(f * lanes, (f + 1) * lanes)
                pieces.append(ox[:, sl] * jnp.broadcast_to(row, (half, lanes)).astype(BF))
            parts.append(jnp.concatenate(pieces, axis=1))
        spread = jnp.concatenate(parts, axis=0)
        g = jnp.dot(spread, wy[...], preferred_element_type=F32).astype(BF)
        first, second = slice(0, lane_pad), slice(lane_pad, 2 * lane_pad)
        gs = jnp.concatenate(
            [jnp.concatenate([g[:half, b], g[half:, b]], axis=1) for b in (first, second)], axis=0
        )
        ar = jnp.dot(gs, fy[0], preferred_element_type=F32).astype(BF)
        ai = jnp.dot(gs, fy[1], preferred_element_type=F32).astype(BF)
        v = pot[p]
        grid = v.shape[0]
        br, bi = [], []
        for b in range(2):
            rows_b = slice(b * half, (b + 1) * half)
            a = jnp.concatenate([ar[rows_b], ai[rows_b]], axis=0)
            psi = jnp.dot(fx[...], a, preferred_element_type=F32)
            w = jnp.concatenate([psi[:grid] * v, psi[grid:] * v], axis=0).astype(BF)
            bk = jnp.dot(fxb[...], w, preferred_element_type=F32).astype(BF)
            br.append(bk[:half])
            bi.append(bk[half:])
        cc = jnp.dot(jnp.concatenate(br, axis=0), fyb[0], preferred_element_type=F32)
        cc = cc + jnp.dot(jnp.concatenate(bi, axis=0), fyb[1], preferred_element_type=F32)
        cc = cc.astype(BF)
        pk = jnp.concatenate(
            [jnp.concatenate([cc[:half, c], cc[half:, c]], axis=1) for c in (first, second)], axis=0
        )
        d = jnp.dot(pk, wyt[...], preferred_element_type=F32)
        for c in range(2):
            s = jnp.sum(d[c * half : (c + 1) * half] * oxf[...], axis=0, keepdims=True)
            for f in range(nf):
                acc[f, pl.ds(2 * p + c, 1), :] = s[:, f * lanes : (f + 1) * lanes]
        return carry

    lax.fori_loop(0, planes, step, 0)
    for f in range(nf):
        out[f] = acc[f].astype(BF)


def sticks_kernel(
    n_fft, n_band, scale, picked, coef, length, square, fzb,
    applied, gathered, recv, send, fft_send, fft_recv, band_send, band_recv,
):
    greet([("fft", n_fft), ("band", n_band)])
    exchange("fft", n_fft, picked, recv, fft_send, fft_recv)
    half = coef.shape[1] // 2
    sticks = coef.shape[0] // 2
    group = sticks // n_band
    values = recv[...].astype(F32).reshape(-1, recv.shape[2])
    local = jnp.dot(fzb[...], values, precision=HIGH, preferred_element_type=F32).T
    live, z_freq = live_of(length[...], half, coef.shape)
    kinetic = (square[...] + z_freq * z_freq).astype(F32) * scale
    h = jnp.where(live, kinetic * coef[...] + local, 0.0)
    applied[...] = h.astype(BF)
    for r in range(n_band):
        one, two = r * group, sticks + r * group
        send[r] = jnp.concatenate([h[one : one + group], h[two : two + group]], axis=0).astype(BF)
    exchange("band", n_band, send, gathered, band_send, band_recv)


def reduce_kernel(n_fft, n_band, part, out, recv, mid, last, fft_send, fft_recv, band_send, band_recv):
    greet([("fft", n_fft), ("band", n_band)])
    exchange("fft", n_fft, part, recv, fft_send, fft_recv)
    total = recv[0]
    for f in range(1, n_fft):
        total = total + recv[f]
    for r in range(n_band):
        mid[r] = total[r : r + 1]
    exchange("band", n_band, mid, last, band_send, band_recv)
    total = last[0]
    for r in range(1, n_band):
        total = total + last[r]
    out[...] = total


def dma(n):
    return pltpu.SemaphoreType.DMA((n,))


def per_device(n_band, n_fft, band_coeffs, potential, stick_column, stick_length, orbitals):
    bands, sticks, width = band_coeffs.shape
    half = width // 2
    grid = potential.shape[1]
    planes = potential.shape[0]
    fy, fx, fxb, fyb, fz, fzb = dft_tables(half, grid)
    coef = band_coeffs.reshape(bands * sticks, width)
    first = lax.axis_index("fft") * sticks
    own = lax.dynamic_slice_in_dim(stick_column, first, sticks)
    x_freq = own // half - half // 2
    y_freq = own % half - half // 2
    square = jnp.tile(x_freq**2 + y_freq**2, bands)[:, None]
    length = jnp.tile(stick_length, bands)[:, None]
    block = (n_fft, 2 * planes, bands * sticks)

    def params(cid):
        return pltpu.CompilerParams(collective_id=cid, has_side_effects=True)

    recv = pl.pallas_call(
        functools.partial(columns_kernel, n_fft),
        out_shape=jax.ShapeDtypeStruct(block, BF),
        in_specs=[VM] * 3,
        out_specs=VM,
        scratch_shapes=[pltpu.VMEM(block, BF), dma(n_fft), dma(n_fft)],
        compiler_params=params(0),
        name="columns",
    )(coef, length, jnp.asarray(fz, F32))

    flat = n_fft * bands * sticks
    picked = pl.pallas_call(
        functools.partial(planes_kernel, half),
        out_shape=jax.ShapeDtypeStruct(block, BF),
        in_specs=[VM] * 7,
        out_specs=VM,
        scratch_shapes=[
            pltpu.VMEM((half, flat), BF),
            pltpu.VMEM((half, flat), F32),
            pltpu.VMEM((fy.shape[1], flat), BF),
            pltpu.VMEM((flat, fy.shape[1]), BF),
            pltpu.VMEM(block, F32),
            pltpu.VMEM(block, F32),
        ],
        compiler_params=pltpu.CompilerParams(vmem_limit_bytes=48 * 1024 * 1024),
        name="planes",
    )(
        recv, potential, stick_column.reshape(n_fft, sticks),
        jnp.asarray(fy, BF), jnp.asarray(fx, BF), jnp.asarray(fxb, BF), jnp.asarray(fyb, BF),
    )

    group = sticks // n_band
    swap = (n_band, bands * group, width)
    applied, gathered = pl.pallas_call(
        functools.partial(sticks_kernel, n_fft, n_band, 2.0 / (half * half)),
        out_shape=(jax.ShapeDtypeStruct(coef.shape, BF), jax.ShapeDtypeStruct(swap, BF)),
        in_specs=[VM] * 5,
        out_specs=(VM, VM),
        scratch_shapes=[
            pltpu.VMEM(block, BF), pltpu.VMEM(swap, BF),
            dma(n_fft), dma(n_fft), dma(n_band), dma(n_band),
        ],
        compiler_params=params(1),
        name="sticks",
    )(picked, coef, length, square, jnp.asarray(fzb, F32))

    gathered = gathered.reshape(n_band * bands, group, width)
    swapped = jnp.concatenate([gathered[:, :, half:], -gathered[:, :, :half]], 2)
    stacked = jnp.concatenate([gathered, swapped], 0).reshape(2 * n_band * bands, -1)
    partial = lax.dot_general(
        orbitals.reshape(orbitals.shape[0], -1), stacked, (((1,), (1,)), ((), ())),
        preferred_element_type=F32,
    )
    owned = orbitals.shape[0] // (n_band * n_fft) * partial.shape[1]
    partial = partial.reshape(n_band, n_fft, owned).transpose(1, 0, 2)
    margin = pl.pallas_call(
        functools.partial(reduce_kernel, n_fft, n_band),
        out_shape=jax.ShapeDtypeStruct((1, owned), F32),
        in_specs=[VM],
        out_specs=VM,
        scratch_shapes=[
            pltpu.VMEM(partial.shape, F32),
            pltpu.VMEM((n_band, 1, owned), F32), pltpu.VMEM((n_band, 1, owned), F32),
            dma(n_fft), dma(n_fft), dma(n_band), dma(n_band),
        ],
        compiler_params=params(2),
        name="reduce",
    )(partial)
    return applied.reshape(band_coeffs.shape), margin.reshape(-1, 2 * n_band * bands)


def solution(mesh):
    placed = (
        P("band", "fft", None),
        P("fft", None, None),
        P(),
        P("fft"),
        P(None, ("band", "fft"), None),
    )
    return jax.shard_map(
        functools.partial(per_device, mesh.shape["band"], mesh.shape["fft"]),
        mesh=mesh,
        in_specs=placed,
        out_specs=(P("band", "fft", None), P(("band", "fft"), None)),
        check_vma=False,
    )
```

time: 326 us -> 83 us (0.25); the launches traced: 321 us -> 82.5 us
  waiting for transfers between devices: 142 us -> 0 us
  matrix products: 78.6 us -> 0.43 us
  Pallas kernels: 0 us -> 65.5 us
  local copies, waits for them, and re-layouts: 42.6 us -> 13.6 us
  starting transfers between devices: 22.7 us -> 0 us
  between operations: 14.8 us -> 0.73 us
  blocking collectives: 13.9 us -> 0 us
    unnamed x2 -> x0, waiting for transfers between devices: 136 us -> none
    dot_general x61 -> x1, matrix products: 78.6 us -> 0.43 us  [per_device(): lax.dot_general(orbitals.reshape(orbitals.shape[0], -1), stacked, (((1,),...]
    pallas_call x0 -> x4, Pallas kernels: none -> 65.5 us  [the longest x1 23.9 us: per_device(): pl.pallas_call(functools.partial(planes_kernel, half), out_shape=jax.Shap...]
    all_to_all x4 -> x0, starting transfers between devices: 22.6 us -> none  [the longest x2 11.6 us: apply_hamiltonian(): lax.all_to_all(picked.astype(jnp.bfloat16), 'fft', split_axis=3, concat_a...]
    mul x24 -> x0, local copies, waits for them, and re-layouts: 16.8 us -> none  [place_plane(): spread = plane_vals[..., None] * onehot_y]
    all_to_all x1 -> x0, blocking collectives: 13.9 us -> none  [per_device(): lax.all_to_all(applied, 'band', split_axis=1, concat_axis=0, tiled=True)]
    dynamic_update_slice x24 -> x0, local copies, waits for them, and re-layouts: 7.41 us -> none  [apply_hamiltonian(): picked = lax.map(pick_plane, jnp.moveaxis(freq_box, 2, 0))]
    all_to_all x4 -> x0, waiting for transfers between devices: 5.59 us -> none  [the longest x2 3.1 us: apply_hamiltonian(): lax.all_to_all(columns.astype(jnp.bfloat16), 'fft', split_axis=2, concat_...]
  transfers between devices with their start and end apart: 5 -> 0, of which waited for: 3 -> 0; matrix products, arithmetic and copies ran while one was open for 36% -> 0% of each run, Pallas kernels for 0% -> 0%
where the time goes in v1:
time: 83 us; the launch traced here: 82.5 us
  Pallas kernels  65.5 us (79%)
  local copies, waits for them, and re-layouts  13.6 us (16%)
  other arithmetic  2.18 us (3%)
    pallas_call x1, Pallas kernels, per_device(): pl.pallas_call(functools.partial(planes_kernel, half), out_shape=jax.Shap...  23.9 us
    pallas_call x1, Pallas kernels, per_device(): pl.pallas_call(functools.partial(sticks_kernel, n_fft, n_band, 2.0 / (hal...  17 us
    pallas_call x1, Pallas kernels, per_device(): pl.pallas_call(functools.partial(reduce_kernel, n_fft, n_band), out_shape...  13.7 us
    pallas_call x1, Pallas kernels, per_device(): pl.pallas_call(functools.partial(columns_kernel, n_fft), out_shape=jax.Sh...  11 us
    unnamed x19, local copies, waits for them, and re-layouts  7.54 us

profile of v1, /device:TPU:1, one launch (start us, length us, event | category | flops | bytes accessed | tf_op | source)
XLA Modules:
  0.0 82.5 jit_solution(15060780991921732749)
XLA Ops:
  0.6 0.8 tile.4
  1.4 0.8 broadcast_in_dim_tile.9.length
  2.2 11.0 %columns.1.recv = bf16[16,24,128]{2,1,0:T(8,128)(2,1)} custom-call(f32[128,192]{1,0:T(8,128)} %bitcast.11, s32[128,1]{1,0:T(8,128)} %broadcast_in_dim_tile.9.length, f32[384,192]{1,0:T(8,128)} %constant.45.clone.fz), custom_call_target="tpu_custom_call" | custom-call | tf_op jit(solution)/shard_map/columns/pallas_call | solution.py:218
  13.2 0.8 reshape.27.col
  13.9 1.7 %copy-done.1 = f32[12,192,192]{2,1,0:T(8,128)S(1)} copy-done((f32[12,192,192]{2,1,0:T(8,128)S(1)}, f32[12,192,192]{2,1,0:T(8,128)}, u32[]{:S(2)}) %copy-start.1) | copy-done | bytes 1769496
  15.6 0.9 %copy-done.3 = bf16[16,24,128]{2,1,0:T(8,128)(2,1)S(1)} copy-done((bf16[16,24,128]{2,1,0:T(8,128)(2,1)S(1)}, bf16[16,24,128]{2,1,0:T(8,128)(2,1)}, u32[]{:S(2)}) %copy-start.3) | copy-done | bytes 98328
  16.5 0.9 %copy-done.4 = bf16[2,256,192]{2,1,0:T(8,128)(2,1)S(1)} copy-done((bf16[2,256,192]{2,1,0:T(8,128)(2,1)S(1)}, bf16[2,256,192]{2,1,0:T(8,128)(2,1)}, u32[]{:S(2)}) %copy-start.4) | copy-done | bytes 196632
  17.4 0.9 %copy-done.5 = bf16[384,192]{1,0:T(8,128)(2,1)S(1)} copy-done((bf16[384,192]{1,0:T(8,128)(2,1)S(1)}, bf16[384,192]{1,0:T(8,128)(2,1)}, u32[]{:S(2)}) %copy-start.5) | copy-done | bytes 147480
  18.4 0.9 %copy-done.6 = bf16[2,192,256]{2,1,0:T(8,128)(2,1)S(1)} copy-done((bf16[2,192,256]{2,1,0:T(8,128)(2,1)S(1)}, bf16[2,192,256]{2,1,0:T(8,128)(2,1)}, u32[]{:S(2)}) %copy-start.6) | copy-done | bytes 196632
  19.3 0.9 %copy-done.7 = bf16[192,384]{1,0:T(8,128)(2,1)S(1)} copy-done((bf16[192,384]{1,0:T(8,128)(2,1)S(1)}, bf16[192,384]{1,0:T(8,128)(2,1)}, u32[]{:S(2)}) %copy-start.7) | copy-done | bytes 147480
  20.2 23.9 %planes.1.picked = bf16[16,24,128]{2,1,0:T(8,128)(2,1)S(1)} custom-call(bf16[16,24,128]{2,1,0:T(8,128)(2,1)S(1)} %copy-done.3, f32[12,192,192]{2,1,0:T(8,128)S(1)} %copy-done.1, s32[16,64]{1,0:T(8,128)S(1)} %reshape.27.col, bf16[2,256,192]{2,1,0:T(8,128)(2,1)S(1)} %copy-done.4, bf16[384,192]{1,0:T(8,128)(2,1)S(1)} %copy-done.5, ...), custom_call_target="tpu_custom_call" | custom-call | tf_op jit(solution)/shard_map/planes/pallas_call | solution.py:229
  44.1 0.6 copy-done.2
  44.7 0.8 fusion.7
  45.5 0.8 broadcast_in_dim_tile.8.square
  46.2 17.0 %sticks.1 = (bf16[128,192]{1,0:T(8,128)(2,1)}, bf16[8,16,192]{2,1,0:T(8,128)(2,1)}) custom-call(bf16[16,24,128]{2,1,0:T(8,128)(2,1)} %copy-done.2, f32[128,192]{1,0:T(8,128)} %bitcast.12, s32[128,1]{1,0:T(8,128)} %broadcast_in_dim_tile.9.length, s32[128,1]{1,0:T(8,128)} %broadcast_in_dim_tile.8.square, f32[192,384]{1,0:T(8,128)} %constant.50.clone.fzb), custom_call_target="tpu_custom_call" | custom-call | tf_op jit(solution)/shard_map/sticks/pallas_call | solution.py:251
  63.3 0.9 %copy.24 = bf16[16,8,192]{2,0,1:T(8,128)(2,1)S(1)} copy(bf16[16,8,192]{2,1,0:T(8,128)(2,1)} %bitcast.15) | data formatting | bytes 98304 | tf_op jit(solution)/shard_map/reshape | solution.py:264
  64.2 0.4 convolution_bitcast_fusion
  64.7 0.1 copy.25
  64.9 0.7 copy.28
  65.6 13.7 %reduce.5 = f32[1,128]{1,0:T(1,128)} custom-call(f32[16,8,128]{2,1,0:T(8,128)} %bitcast.13), custom_call_target="tpu_custom_call" | custom-call | tf_op jit(solution)/shard_map/reduce/pallas_call | solution.py:273
  79.3 0.5 broadcast.15
  79.8 1.3 %reduce.4 = f32[128]{0:T(128)S(1)} reduce(f32[1,128]{1,0:T(1,128)} %reduce.5, f32[]{:T(128)} %broadcast.15), dimensions={0}, to_apply=%pallas_call.19.reduce_sub_computation.3 | reduce | bytes 1028 | tf_op jit(solution)/shard_map/reduce/pallas_call | solution.py:273
  81.2 0.7 reshape.31
  81.8 0.6 copy.30
  (14 shorter events, 0.2 us)
Async XLA Ops:
  0.6 63.6 %copy-start = (bf16[512,8,192]{0,2,1:T(8,128)(2,1)S(1)}, bf16[512,8,192]{0,2,1:T(8,128)(2,1)}, u32[]{:S(2)}) copy-start(bf16[512,8,192]{0,2,1:T(8,128)(2,1)} %param.15) | copy-start | bytes 4718596
  13.9 1.7 %copy-start.1 = (f32[12,192,192]{2,1,0:T(8,128)S(1)}, f32[12,192,192]{2,1,0:T(8,128)}, u32[]{:S(2)}) copy-start(f32[12,192,192]{2,1,0:T(8,128)} %pot.1) | copy-start | bytes 5308420
  15.6 0.9 %copy-start.3 = (bf16[16,24,128]{2,1,0:T(8,128)(2,1)S(1)}, bf16[16,24,128]{2,1,0:T(8,128)(2,1)}, u32[]{:S(2)}) copy-start(bf16[16,24,128]{2,1,0:T(8,128)(2,1)} %columns.1.recv) | copy-start | bytes 294916
  16.5 0.9 %copy-start.4 = (bf16[2,256,192]{2,1,0:T(8,128)(2,1)S(1)}, bf16[2,256,192]{2,1,0:T(8,128)(2,1)}, u32[]{:S(2)}) copy-start(bf16[2,256,192]{2,1,0:T(8,128)(2,1)} %constant.46.clone.fy) | copy-start | bytes 589828
  17.4 0.9 %copy-start.5 = (bf16[384,192]{1,0:T(8,128)(2,1)S(1)}, bf16[384,192]{1,0:T(8,128)(2,1)}, u32[]{:S(2)}) copy-start(bf16[384,192]{1,0:T(8,128)(2,1)} %constant.47.clone.fx) | copy-start | bytes 442372
  18.4 0.9 %copy-start.6 = (bf16[2,192,256]{2,1,0:T(8,128)(2,1)S(1)}, bf16[2,192,256]{2,1,0:T(8,128)(2,1)}, u32[]{:S(2)}) copy-start(bf16[2,192,256]{2,1,0:T(8,128)(2,1)} %constant.49.clone.fyb) | copy-start | bytes 589828
  19.3 0.9 %copy-start.7 = (bf16[192,384]{1,0:T(8,128)(2,1)S(1)}, bf16[192,384]{1,0:T(8,128)(2,1)}, u32[]{:S(2)}) copy-start(bf16[192,384]{1,0:T(8,128)(2,1)} %constant.48.clone.fxb) | copy-start | bytes 442372
  44.1 0.6 copy-start.2
  63.2 18.6 %copy-start.8 = (bf16[128,192]{1,0:T(8,128)(2,1)S(1)}, bf16[128,192]{1,0:T(8,128)(2,1)}, u32[]{:S(2)}) copy-start(bf16[128,192]{1,0:T(8,128)(2,1)} %get-tuple-element.4) | copy-start | bytes 147460

commit v2 on v0

v2 whole, which is shorter than its diff:
```python
import functools
import math

import jax
import jax.numpy as jnp
import numpy as np
from jax import lax
from jax.experimental import pallas as pl
from jax.experimental.pallas import tpu as pltpu
from jax.sharding import PartitionSpec as P

BF = jnp.bfloat16
F32 = jnp.float32
I32 = jnp.int32
MESH = pl.DeviceIdType.MESH
LANES = 128
SUB = 8


def dft_tables(half, grid):
    freq = np.arange(half) - half // 2
    angle = (freq[:, None] * np.arange(grid)[None, :] % grid) * (2.0 * math.pi / grid)
    co, si = np.cos(angle), np.sin(angle)
    cp, sp = (np.concatenate([a, np.zeros((LANES - half, grid))], 0) for a in (co, si))
    near, far = slice(0, LANES), slice(LANES, grid)

    def ahead(part):
        return (np.concatenate([cp[:, part], -sp[:, part]], 0),
                np.concatenate([sp[:, part], cp[:, part]], 0))

    def back(part):
        return (np.concatenate([cp[:, part].T, -sp[:, part].T], 1),
                np.concatenate([sp[:, part].T, cp[:, part].T], 1))

    y_near = np.concatenate(ahead(near), 1)
    r, i = ahead(far)
    o = np.zeros_like(r)
    y_far = np.concatenate([np.concatenate([r, o, i, o], 1), np.concatenate([o, r, o, i], 1)], 0)
    x_ahead = np.concatenate(
        [np.concatenate([co.T, -si.T], 1), np.concatenate([si.T, co.T], 1)], 0)
    x_back = np.concatenate([np.concatenate([co, si], 1), np.concatenate([-si, co], 1)], 0)
    yb_near = np.concatenate(back(near), 0)
    r, i = back(far)
    o = np.zeros_like(r)
    yb_far = np.concatenate([np.concatenate([r, o, i, o], 0), np.concatenate([o, r, o, i], 0)], 1)
    z_ahead = np.stack(
        [np.concatenate([co.T, -si.T], 1), np.concatenate([si.T, co.T], 1)], 1
    ).reshape(2 * grid, 2 * half)
    z_back = np.concatenate(
        [np.stack([co, si], -1).reshape(half, -1), np.stack([-si, co], -1).reshape(half, -1)], 0
    ) / float(grid) ** 3

    def two_part(a):
        high = a.astype(np.float32).astype(BF)
        low = (a - high.astype(np.float64)).astype(np.float32).astype(BF)
        return np.stack([high, low])

    plain = [a.astype(np.float32).astype(BF) for a in (y_near, y_far, x_ahead, x_back, yb_near, yb_far)]
    return [two_part(z_ahead)] + plain + [two_part(z_back)]


def dot(a, b):
    return jnp.dot(a, b, preferred_element_type=F32)


def dot_t(a, b):
    return lax.dot_general(a, b, (((1,), (1,)), ((), ())), preferred_element_type=F32)


def iota(shape, dim):
    return lax.broadcasted_iota(I32, shape, dim)


def join(parts, axis):
    return jnp.concatenate(parts, axis=axis)


class Exchange:
    def __init__(self, axis, n, src, dst, send_sem, recv_sem):
        me = lax.axis_index(axis)
        self.copies = []
        for k in range(1, n):
            peer = lax.rem(me + k, n)
            self.copies.append(pltpu.make_async_remote_copy(
                src_ref=src.at[peer], dst_ref=dst.at[me],
                send_sem=send_sem.at[k], recv_sem=recv_sem.at[k],
                device_id={axis: peer}, device_id_type=MESH))
        self.own = pltpu.make_async_copy(src.at[me], dst.at[me], send_sem.at[0])

    def start(self):
        for copy in self.copies:
            copy.start()
        self.own.start()

    def wait(self):
        self.own.wait()
        for copy in self.copies:
            copy.wait()


def build_cells(half, q, w1, w1t, oxl):
    qq = q[...]
    xs = qq // half
    ys = qq - xs * half
    xh = xs // SUB
    xl = xs - xh * SUB
    cell = xh * LANES + ys
    down = cell.astype(F32).T
    cells, rows = w1t.shape[0], qq.shape[0]
    for k in range(rows):
        sl = slice(LANES * k, LANES * (k + 1))
        w1t[:, sl] = (iota((cells, LANES), 0) == cell[k : k + 1, :]).astype(F32).astype(BF)
        w1[sl, :] = (iota((LANES, cells), 1).astype(F32) == down[:, k : k + 1]).astype(F32).astype(BF)
        oxl[:, sl] = (iota((SUB, LANES), 0) == xl[k : k + 1, :]).astype(F32)


def spread_sticks(recv, oxl, cfb, lhs):
    nf, rows, lanes = recv.shape
    low = iota((rows, lanes), 1) < lanes // 2
    for k in range(nf // 2):
        a = recv[2 * k].astype(F32)
        b = recv[2 * k + 1].astype(F32)
        sl = slice(lanes * k, lanes * (k + 1))
        cfb[0, :, sl] = jnp.where(low, a, pltpu.roll(b, lanes // 2, 1))
        cfb[1, :, sl] = jnp.where(low, pltpu.roll(a, lanes // 2, 1), b)
    count = cfb.shape[2]
    for p in range(rows // 2):
        blk = [
            oxl[...] * jnp.broadcast_to(cfb[b, 2 * p + c : 2 * p + c + 1, :], (SUB, count))
            for b in range(2) for c in range(2)
        ]
        lhs[4 * SUB * p : 4 * SUB * (p + 1), :] = join(blk, 0).astype(BF)


def place(lhs, w1, gbox):
    blocks, half, _ = gbox.shape
    for t in range(half // (2 * SUB)):
        o = dot(lhs[...], w1[:, 2 * LANES * t : 2 * LANES * (t + 1)])
        o = join([o[:, :LANES].reshape(blocks, SUB, LANES), o[:, LANES:].reshape(blocks, SUB, LANES)], 1)
        gbox[:, 2 * SUB * t : 2 * SUB * (t + 1), :] = o.astype(BF)


def apply_potential(first, count, gbox, pot, fya, fyb, fx, fxb, ya, yb, pk):
    half, grid = gbox.shape[1], pot.shape[1]
    wide = 3 * LANES
    planes = range(count)
    ls = []
    for d in planes:
        base = 4 * (first + d)
        for b in range(2):
            ls.append(join([gbox[base + 2 * b], gbox[base + 2 * b + 1]], 1))
    near = dot(join(ls, 0), fya[...]).astype(BF)
    far = dot(join([join([ls[2 * d], ls[2 * d + 1]], 1) for d in planes], 0), fyb[...]).astype(BF)
    cols = []
    for d in planes:
        a0 = near[2 * half * d : 2 * half * d + half]
        a2 = near[2 * half * d + half : 2 * half * (d + 1)]
        a1 = far[half * d : half * (d + 1)]
        for a in (a0, a1, a2):
            cols.append(join([a[:, :LANES], a[:, LANES:]], 0))
    psi = dot(fx[...], join(cols, 1))
    vs = []
    for d in planes:
        v = pot[first + d]
        v0, v1 = v[:, :LANES], v[:, LANES:]
        vs += [v0, join([v1, v1], 1), v0]
    vv = join(vs, 1)
    w = join([psi[:grid] * vv, psi[grid:] * vv], 0).astype(BF)
    bb = dot(fxb[...], w).astype(BF)
    p1, p2 = [], []
    for d in planes:
        def piece(j):
            sl = slice(wide * d + LANES * j, wide * d + LANES * (j + 1))
            return join([bb[:half, sl], bb[half:, sl]], 1)
        p1 += [piece(0), piece(2)]
        p2.append(piece(1))
    c1 = dot(join(p1, 0), ya[...])
    c2 = dot(join(p2, 0), yb[...])
    per_band = pk.shape[0] // 2
    for d in planes:
        for b in range(2):
            at = 2 * half * d + half * b
            cc = c1[at : at + half] + c2[half * d : half * (d + 1), 2 * LANES * b : 2 * LANES * (b + 1)]
            rows = [
                join([cc[SUB * h : SUB * (h + 1), LANES * c : LANES * (c + 1)] for h in range(half // SUB)], 1)
                for c in range(2)
            ]
            to = per_band * b + 2 * SUB * (first + d)
            pk[to : to + 2 * SUB, :] = join(rows, 0).astype(BF)


def pick(pk, w1t, oxl, out):
    rows = pk.shape[0]
    blocks = rows // SUB
    per_band = blocks // 2
    ones = (iota((blocks, rows), 1) // SUB == iota((blocks, rows), 0)).astype(F32).astype(BF)
    low = iota((per_band, LANES), 1) < LANES // 2
    step = 2 * LANES
    for t in range(w1t.shape[1] // step):
        sl = slice(step * t, step * (t + 1))
        d = dot(pk[...], w1t[:, sl])
        m = (d.reshape(blocks, SUB, step) * oxl[:, sl][None]).reshape(rows, step).astype(BF)
        s = dot(ones, m)
        for h in range(2):
            lanes = slice(LANES * h, LANES * (h + 1))
            d0, d1 = s[:per_band, lanes], s[per_band:, lanes]
            out[4 * t + 2 * h] = jnp.where(low, d0, pltpu.roll(d1, LANES // 2, 1)).astype(BF)
            out[4 * t + 2 * h + 1] = jnp.where(low, pltpu.roll(d0, LANES // 2, 1), d1).astype(BF)


def kernel(
    n_band, n_fft, coef_h, pot_h, col_h, len_h, orb_h, fz_h, fya_h, fyb_h, fx_h, fxb_h, ya_h, yb_h, fzb_h,
    applied, margin,
    coef, pot, q, length, orb, fz, fya, fyb, fx, fxb, ya, yb, fzb,
    w1, w1t, oxl, cfb, lhs, gbox, pk,
    send1, recv1, send2, recv2, send3, recv3, send4, recv4, send5, recv5,
    load_sem, fft_send, fft_recv, band_send, band_recv,
):
    loads = {}
    order = [
        (len_h, length.at[0])] + [
        (col_h.at[pl.ds(LANES * k, LANES)], q.at[k]) for k in range(q.shape[0])] + [
        (coef_h, coef), (fz_h, fz), (pot_h, pot), (fya_h, fya), (fyb_h, fyb), (fx_h, fx), (fxb_h, fxb),
        (ya_h, ya), (yb_h, yb), (orb_h, orb), (fzb_h, fzb)]
    for n, (src, dst) in enumerate(order):
        loads[n] = pltpu.make_async_copy(src, dst, load_sem.at[n])
        loads[n].start()
    nq = q.shape[0]

    barrier = pltpu.get_barrier_semaphore()
    for axis, n in (("fft", n_fft), ("band", n_band)):
        me = lax.axis_index(axis)
        for k in range(1, n):
            pl.semaphore_signal(
                barrier, inc=1, device_id={axis: lax.rem(me + k, n)}, device_id_type=MESH)
    exchanges = [
        Exchange("fft", n_fft, send1, recv1, fft_send.at[0], fft_recv.at[0]),
        Exchange("fft", n_fft, send2, recv2, fft_send.at[1], fft_recv.at[1]),
        Exchange("band", n_band, send3, recv3, band_send.at[0], band_recv.at[0]),
        Exchange("fft", n_fft, send4, recv4, fft_send.at[2], fft_recv.at[2]),
        Exchange("band", n_band, send5, recv5, band_send.at[1], band_recv.at[1]),
    ]

    bands, sticks, width = coef.shape
    half = width // 2
    for n in range(nq + 3):
        loads[n].wait()
    me = lax.axis_index("fft")
    row = jnp.sum(jnp.where(iota(q.shape, 0) == me // 2, q[...], 0), axis=0, keepdims=True)
    row = jnp.broadcast_to(row, (SUB, LANES))
    turned = pltpu.roll(row, sticks, 1)
    low = iota((SUB, LANES), 1) < sticks
    row = jnp.where(low == (lax.rem(me, 2) == 0), row, turned)
    x_freq = row // half
    y_freq = row - x_freq * half - half // 2
    x_freq = x_freq - half // 2
    size = join([length[...]] * bands, 1)
    size = jnp.broadcast_to(size, (SUB, LANES))
    below = size // 2
    which = iota((SUB, LANES), 0)
    rows = jnp.where(which == 0, -below, jnp.where(which == 1, size - below, x_freq * x_freq + y_freq * y_freq))
    down = rows.astype(F32).T
    z_freq = iota((bands * sticks, width), 1)
    z_freq = (jnp.where(z_freq >= half, z_freq - half, z_freq) - half // 2).astype(F32)
    live = (z_freq >= down[:, 0:1]) & (z_freq < down[:, 1:2])
    masked = jnp.where(live, coef[...].reshape(bands * sticks, width), 0.0)
    high = masked.astype(BF)
    rest = (masked - high.astype(F32)).astype(BF)
    columns = dot_t(fz[0], high) + (dot_t(fz[0], rest) + dot_t(fz[1], high))
    send1[...] = columns.reshape(send1.shape).astype(BF)
    pl.semaphore_wait(barrier, n_fft + n_band - 2)
    exchanges[0].start()

    build_cells(half, q, w1, w1t, oxl)
    for n in range(nq + 3, len(order)):
        loads[n].wait()
    exchanges[0].wait()

    spread_sticks(recv1, oxl, cfb, lhs)
    place(lhs, w1, gbox)
    count = 4
    for first in range(0, pot.shape[0], count):
        apply_potential(first, count, gbox, pot, fya, fyb, fx, fxb, ya, yb, pk)
    pick(pk, w1t, oxl, send2)
    exchanges[1].start()

    exchanges[1].wait()

    values = recv2[...].reshape(-1, bands * sticks)
    local = (dot(fzb[0], values) + dot(fzb[1], values)).T
    kinetic = (down[:, 2:3] + z_freq * z_freq) * (2.0 / (half * half))
    h = jnp.where(live, kinetic * masked + local, 0.0)
    group = sticks // n_band
    for r in range(n_band):
        one, two = r * group, sticks + r * group
        send3[r] = join([h[one : one + group], h[two : two + group]], 0).astype(BF)
    exchanges[2].start()
    applied[...] = h.astype(BF).reshape(applied.shape)
    exchanges[2].wait()

    ours = recv3[...].astype(F32).reshape(n_band * bands, group, width)
    both = join([ours, join([ours[:, :, half:], -ours[:, :, :half]], 2)], 0)
    total = None
    for j in range(group):
        term = dot(both[:, j, :].astype(BF), orb[j])
        total = term if total is None else total + term
    total = total.T
    per = total.shape[0] // (n_band * n_fft)
    total = total.reshape(n_band, n_fft * per, total.shape[1])
    total = join([total[r] for r in range(n_band)], 1)
    for f in range(n_fft):
        send4[f] = total[per * f : per * (f + 1)]
    exchanges[3].start()
    exchanges[3].wait()
    total = recv4[0]
    for f in range(1, n_fft):
        total = total + recv4[f]
    cols = margin.shape[1]
    for r in range(n_band):
        send5[r] = total[:, cols * r : cols * (r + 1)]
    exchanges[4].start()
    exchanges[4].wait()
    total = recv5[0]
    for r in range(1, n_band):
        total = total + recv5[r]
    margin[...] = total


def per_device(n_band, n_fft, band_coeffs, potential, stick_column, stick_length, orbitals):
    bands, sticks, width = band_coeffs.shape
    half = width // 2
    planes, grid = potential.shape[:2]
    rows = orbitals.shape[0]
    orbitals = orbitals.transpose(1, 2, 0)
    tables = dft_tables(half, grid)
    count, group = stick_column.shape[0], orbitals.shape[0]
    per = rows // (n_band * n_fft)
    cells = half // SUB * LANES
    blocks = planes * bands * 2
    first = (n_fft, 2 * planes, bands * sticks)
    swap = (n_band, bands * group, width)
    cols = 2 * n_band * bands
    fold = (n_fft, per, n_band * cols)
    last = (n_band, per, cols)
    vm, sem = pltpu.VMEM, pltpu.SemaphoreType.DMA
    n_rows = count // LANES
    return pl.pallas_call(
        functools.partial(kernel, n_band, n_fft),
        out_shape=(
            jax.ShapeDtypeStruct(band_coeffs.shape, BF), jax.ShapeDtypeStruct((per, cols), F32)),
        in_specs=[pl.BlockSpec(memory_space=pl.ANY)] * 13,
        out_specs=(pl.BlockSpec(memory_space=pltpu.VMEM),) * 2,
        scratch_shapes=[
            vm(band_coeffs.shape, F32), vm(potential.shape, F32), vm((n_rows, LANES), I32),
            vm((1, sticks), I32), vm(orbitals.shape, BF)]
        + [vm(t.shape, BF) for t in tables]
        + [
            vm((count, cells), BF), vm((cells, count), BF), vm((SUB, count), F32),
            vm((bands, 2 * planes, count), F32), vm((SUB * blocks, count), BF),
            vm((blocks, half, LANES), BF), vm((SUB * blocks, cells), BF)]
        + [vm(first, BF)] * 4 + [vm(swap, BF)] * 2 + [vm(fold, F32)] * 2 + [vm(last, F32)] * 2
        + [sem((n_rows + 12,)), sem((3, n_fft)), sem((3, n_fft)), sem((2, n_band)), sem((2, n_band))],
        compiler_params=pltpu.CompilerParams(
            collective_id=0, has_side_effects=True, vmem_limit_bytes=60 * 1024 * 1024),
        name="hamiltonian",
    )(band_coeffs, potential, stick_column, stick_length, orbitals, *[jnp.asarray(t) for t in tables])


def solution(mesh):
    placed = (
        P("band", "fft", None),
        P("fft", None, None),
        P(),
        P("fft"),
        P(None, ("band", "fft"), None),
    )
    return jax.shard_map(
        functools.partial(per_device, mesh.shape["band"], mesh.shape["fft"]),
        mesh=mesh,
        in_specs=placed,
        out_specs=(P("band", "fft", None), P(("band", "fft"), None)),
        check_vma=False,
    )
```

time: 326 us -> 45.4 us (0.14); the launches traced: 321 us -> 45.2 us
  waiting for transfers between devices: 142 us -> 0 us
  matrix products: 78.6 us -> 0 us
  Pallas kernels: 0 us -> 41.9 us
  local copies, waits for them, and re-layouts: 42.6 us -> 2.72 us
  starting transfers between devices: 22.7 us -> 0 us
  between operations: 14.8 us -> 0.64 us
  blocking collectives: 13.9 us -> 0 us
  other arithmetic: 4.97 us -> 0 us
    unnamed x2 -> x0, waiting for transfers between devices: 136 us -> none
    dot_general x61 -> x0, matrix products: 78.6 us -> none  [the longest x24 20 us: pick_plane(): jnp.einsum('xs,bcxy->bcsy', onehot_x, plane_box, precision=HIGHEST_MODE)]
    pallas_call x0 -> x1, Pallas kernels: none -> 41.9 us  [per_device(): pl.pallas_call(functools.partial(kernel, n_band, n_fft), out_shape=(jax.S...]
    all_to_all x4 -> x0, starting transfers between devices: 22.6 us -> none  [the longest x2 11.6 us: apply_hamiltonian(): lax.all_to_all(picked.astype(jnp.bfloat16), 'fft', split_axis=3, concat_a...]
    mul x24 -> x0, local copies, waits for them, and re-layouts: 16.8 us -> none  [place_plane(): spread = plane_vals[..., None] * onehot_y]
    all_to_all x1 -> x0, blocking collectives: 13.9 us -> none  [per_device(): lax.all_to_all(applied, 'band', split_axis=1, concat_axis=0, tiled=True)]
    unnamed x33 -> x2, local copies, waits for them, and re-layouts: 11.1 us -> 2.72 us
    dynamic_update_slice x24 -> x0, local copies, waits for them, and re-layouts: 7.41 us -> none  [apply_hamiltonian(): picked = lax.map(pick_plane, jnp.moveaxis(freq_box, 2, 0))]
  transfers between devices with their start and end apart: 5 -> 0, of which waited for: 3 -> 0; matrix products, arithmetic and copies ran while one was open for 36% -> 0% of each run, Pallas kernels for 0% -> 0%
where the time goes in v2:
time: 45.4 us; the launch traced here: 45.2 us
  Pallas kernels  41.9 us (92%)
  local copies, waits for them, and re-layouts  2.72 us (6%)
  between operations  0.64 us (1%)
    pallas_call x1, Pallas kernels, per_device(): pl.pallas_call(functools.partial(kernel, n_band, n_fft), out_shape=(jax.S...  41.9 us
    unnamed x2, local copies, waits for them, and re-layouts  2.72 us

profile of v2, /device:TPU:1, one launch (start us, length us, event | category | flops | bytes accessed | tf_op | source)
XLA Modules:
  0.0 45.2 jit_solution(6932378771492733371)
XLA Ops:
  0.6 41.9 %hamiltonian.1 = (bf16[2,64,192]{2,1,0:T(8,128)(2,1)}, f32[4,32]{1,0:T(4,128)}) custom-call(f32[2,64,192]{2,1,0:T(8,128)} %coef_h.1, f32[12,192,192]{2,1,0:T(8,128)} %pot_h.1, s32[1024]{0:T(1024)} %col_h.1, s32[64]{0:T(128)} %len_h.1, bf16[8,192,512]{2,1,0:T(8,128)(2,1)} %bitcast.1, bf16[2,384,192]{2,1,0:T(8,128)(2,1)} %constant.16.clone.fz_h, ...), custom_call_target="tpu_custom_call" | custom-call | tf_op jit(solution)/shard_map/hamiltonian/pallas_call | solution.py:347
  42.5 1.5 %copy.17 = bf16[2,64,192]{2,1,0:T(8,128)(2,1)} copy(bf16[2,64,192]{2,1,0:T(8,128)(2,1)} %get-tuple-element.4) | data formatting | bytes 98304
  44.0 1.2 %copy.18 = f32[4,32]{1,0:T(4,128)} copy(f32[4,32]{1,0:T(4,128)} %get-tuple-element.5) | data formatting | bytes 1024

commit v3 on v2

--- a/solution.py
+++ b/solution.py
@@ -36,9 +36,15 @@
     r, i = ahead(far)
     o = np.zeros_like(r)
     y_far = np.concatenate([np.concatenate([r, o, i, o], 1), np.concatenate([o, r, o, i], 1)], 0)
+    order = np.concatenate([np.arange(0, half, 2), np.arange(1, half, 2)])
+    cx, sx = co[order], si[order]
     x_ahead = np.concatenate(
-        [np.concatenate([co.T, -si.T], 1), np.concatenate([si.T, co.T], 1)], 0)
-    x_back = np.concatenate([np.concatenate([co, si], 1), np.concatenate([-si, co], 1)], 0)
+        [np.concatenate([cx.T, -sx.T], 1), np.concatenate([sx.T, cx.T], 1)], 0)
+    parts = []
+    for part in (slice(0, half // 2), slice(half // 2, half)):
+        c, s = cx[part, : grid // 2], sx[part, : grid // 2]
+        parts.append(np.concatenate([np.concatenate([c, s], 1), np.concatenate([-s, c], 1)], 0))
+    x_back = np.stack(parts)
     yb_near = np.concatenate(back(near), 0)
     r, i = back(far)
     o = np.zeros_like(r)
@@ -102,6 +108,7 @@
     qq = q[...]
     xs = qq // half
     ys = qq - xs * half
+    xs = lax.rem(xs, 2) * (half // 2) + xs // 2
     xh = xs // SUB
     xl = xs - xh * SUB
     cell = xh * LANES + ys
@@ -165,8 +172,11 @@
         v0, v1 = v[:, :LANES], v[:, LANES:]
         vs += [v0, join([v1, v1], 1), v0]
     vv = join(vs, 1)
-    w = join([psi[:grid] * vv, psi[grid:] * vv], 0).astype(BF)
-    bb = dot(fxb[...], w).astype(BF)
+    re, im = psi[:grid] * vv, psi[grid:] * vv
+    mid, quarter = grid // 2, half // 2
+    even = dot(fxb[0], join([re[:mid] + re[mid:], im[:mid] + im[mid:]], 0).astype(BF))
+    odd = dot(fxb[1], join([re[:mid] - re[mid:], im[:mid] - im[mid:]], 0).astype(BF))
+    bb = join([even[:quarter], odd[:quarter], even[quarter:], odd[quarter:]], 0).astype(BF)
     p1, p2 = [], []
     for d in planes:
         def piece(j):
@@ -189,7 +199,7 @@
             pk[to : to + 2 * SUB, :] = join(rows, 0).astype(BF)
 
 
-def pick(pk, w1t, oxl, out):
+def pick(pk, w1t, oxl, kept, out):
     rows = pk.shape[0]
     blocks = rows // SUB
     per_band = blocks // 2
@@ -199,13 +209,13 @@
     for t in range(w1t.shape[1] // step):
         sl = slice(step * t, step * (t + 1))
         d = dot(pk[...], w1t[:, sl])
-        m = (d.reshape(blocks, SUB, step) * oxl[:, sl][None]).reshape(rows, step).astype(BF)
-        s = dot(ones, m)
-        for h in range(2):
-            lanes = slice(LANES * h, LANES * (h + 1))
-            d0, d1 = s[:per_band, lanes], s[per_band:, lanes]
-            out[4 * t + 2 * h] = jnp.where(low, d0, pltpu.roll(d1, LANES // 2, 1)).astype(BF)
-            out[4 * t + 2 * h + 1] = jnp.where(low, pltpu.roll(d0, LANES // 2, 1), d1).astype(BF)
+        kept[:, sl] = (d.reshape(blocks, SUB, step) * oxl[:, sl][None]).reshape(rows, step).astype(BF)
+    s = dot(ones, kept[...])
+    for h in range(out.shape[0] // 2):
+        lanes = slice(LANES * h, LANES * (h + 1))
+        d0, d1 = s[:per_band, lanes], s[per_band:, lanes]
+        out[2 * h] = jnp.where(low, d0, pltpu.roll(d1, LANES // 2, 1)).astype(BF)
+        out[2 * h + 1] = jnp.where(low, pltpu.roll(d0, LANES // 2, 1), d1).astype(BF)
 
 
 def kernel(
@@ -216,6 +226,12 @@
     send1, recv1, send2, recv2, send3, recv3, send4, recv4, send5, recv5,
     load_sem, fft_send, fft_recv, band_send, band_recv,
 ):
+    barrier = pltpu.get_barrier_semaphore()
+    for axis, n in (("fft", n_fft), ("band", n_band)):
+        me = lax.axis_index(axis)
+        for k in range(1, n):
+            pl.semaphore_signal(
+                barrier, inc=1, device_id={axis: lax.rem(me + k, n)}, device_id_type=MESH)
     loads = {}
     order = [
         (len_h, length.at[0])] + [
@@ -227,12 +243,6 @@
         loads[n].start()
     nq = q.shape[0]
 
-    barrier = pltpu.get_barrier_semaphore()
-    for axis, n in (("fft", n_fft), ("band", n_band)):
-        me = lax.axis_index(axis)
-        for k in range(1, n):
-            pl.semaphore_signal(
-                barrier, inc=1, device_id={axis: lax.rem(me + k, n)}, device_id_type=MESH)
     exchanges = [
         Exchange("fft", n_fft, send1, recv1, fft_send.at[0], fft_recv.at[0]),
         Exchange("fft", n_fft, send2, recv2, fft_send.at[1], fft_recv.at[1]),
@@ -281,7 +291,7 @@
     count = 4
     for first in range(0, pot.shape[0], count):
         apply_potential(first, count, gbox, pot, fya, fyb, fx, fxb, ya, yb, pk)
-    pick(pk, w1t, oxl, send2)
+    pick(pk, w1t, oxl, lhs, send2)
     exchanges[1].start()
 
     exchanges[1].wait()
@@ -293,12 +303,19 @@
     group = sticks // n_band
     for r in range(n_band):
         one, two = r * group, sticks + r * group
-        send3[r] = join([h[one : one + group], h[two : two + group]], 0).astype(BF)
+        a, b = h[one : one + group], h[two : two + group]
+        tail = join([a[:, LANES:], b[:, LANES:]], 1)
+        send3[r] = join([a[:, :LANES], b[:, :LANES], tail], 0).astype(BF)
     exchanges[2].start()
     applied[...] = h.astype(BF).reshape(applied.shape)
     exchanges[2].wait()
 
-    ours = recv3[...].astype(F32).reshape(n_band * bands, group, width)
+    ours = recv3[...].astype(F32)
+    tail = ours[:, 2 * group :]
+    ours = join([
+        join([ours[:, :group], tail[:, :, : width - LANES]], 2)[:, None],
+        join([ours[:, group : 2 * group], tail[:, :, width - LANES :]], 2)[:, None]], 1)
+    ours = ours.reshape(n_band * bands, group, width)
     both = join([ours, join([ours[:, :, half:], -ours[:, :, :half]], 2)], 0)
     total = None
     for j in range(group):
@@ -338,7 +355,7 @@
     cells = half // SUB * LANES
     blocks = planes * bands * 2
     first = (n_fft, 2 * planes, bands * sticks)
-    swap = (n_band, bands * group, width)
+    swap = (n_band, bands * group * width // LANES, LANES)
     cols = 2 * n_band * bands
     fold = (n_fft, per, n_band * cols)
     last = (n_band, per, cols)

time: 45.4 us -> 43.7 us (0.963)
  Pallas kernels: 41.9 us -> 40.2 us
    pallas_call x1, Pallas kernels: 41.9 us -> 40.2 us  [per_device(): pl.pallas_call(functools.partial(kernel, n_band, n_fft), out_shape=(jax.S...]
where the time goes in v3:
time: 43.7 us; the launch traced here: 43.5 us
  Pallas kernels  40.2 us (92%)
  local copies, waits for them, and re-layouts  2.72 us (6%)
  between operations  0.64 us (1%)
    pallas_call x1, Pallas kernels, per_device(): pl.pallas_call(functools.partial(kernel, n_band, n_fft), out_shape=(jax.S...  40.2 us
    unnamed x2, local copies, waits for them, and re-layouts  2.72 us

profile of v3, /device:TPU:1, one launch (start us, length us, event | category | flops | bytes accessed | tf_op | source)
XLA Modules:
  0.0 43.5 jit_solution(11044065265596746751)
XLA Ops:
  0.6 40.2 %hamiltonian.1 = (bf16[2,64,192]{2,1,0:T(8,128)(2,1)}, f32[4,32]{1,0:T(4,128)}) custom-call(f32[2,64,192]{2,1,0:T(8,128)} %coef_h.1, f32[12,192,192]{2,1,0:T(8,128)} %pot_h.1, s32[1024]{0:T(1024)} %col_h.1, s32[64]{0:T(128)} %len_h.1, bf16[8,192,512]{2,1,0:T(8,128)(2,1)} %bitcast.1, bf16[2,384,192]{2,1,0:T(8,128)(2,1)} %constant.16.clone.fz_h, ...), custom_call_target="tpu_custom_call" | custom-call | tf_op jit(solution)/shard_map/hamiltonian/pallas_call | solution.py:364
  40.8 1.5 %copy.17 = bf16[2,64,192]{2,1,0:T(8,128)(2,1)} copy(bf16[2,64,192]{2,1,0:T(8,128)(2,1)} %get-tuple-element.4) | data formatting | bytes 98304
  42.3 1.2 %copy.18 = f32[4,32]{1,0:T(4,128)} copy(f32[4,32]{1,0:T(4,128)} %get-tuple-element.5) | data formatting | bytes 1024

commit v4 on v3

--- a/solution.py
+++ b/solution.py
@@ -224,7 +224,7 @@
     coef, pot, q, length, orb, fz, fya, fyb, fx, fxb, ya, yb, fzb,
     w1, w1t, oxl, cfb, lhs, gbox, pk,
     send1, recv1, send2, recv2, send3, recv3, send4, recv4, send5, recv5,
-    load_sem, fft_send, fft_recv, band_send, band_recv,
+    kept_h, out_sem, load_sem, fft_send, fft_recv, band_send, band_recv,
 ):
     barrier = pltpu.get_barrier_semaphore()
     for axis, n in (("fft", n_fft), ("band", n_band)):
@@ -307,7 +307,9 @@
         tail = join([a[:, LANES:], b[:, LANES:]], 1)
         send3[r] = join([a[:, :LANES], b[:, :LANES], tail], 0).astype(BF)
     exchanges[2].start()
-    applied[...] = h.astype(BF).reshape(applied.shape)
+    kept_h[...] = h.reshape(kept_h.shape)
+    out_copy = pltpu.make_async_copy(kept_h, applied, out_sem)
+    out_copy.start()
     exchanges[2].wait()
 
     ours = recv3[...].astype(F32)
@@ -332,15 +334,18 @@
     total = recv4[0]
     for f in range(1, n_fft):
         total = total + recv4[f]
-    cols = margin.shape[1]
+    cols = margin.shape[2]
     for r in range(n_band):
         send5[r] = total[:, cols * r : cols * (r + 1)]
     exchanges[4].start()
     exchanges[4].wait()
-    total = recv5[0]
-    for r in range(1, n_band):
-        total = total + recv5[r]
-    margin[...] = total
+    pair = n_band // 2
+    for part in range(2):
+        total = recv5[pair * part]
+        for r in range(pair * part + 1, pair * (part + 1)):
+            total = total + recv5[r]
+        margin[part] = total
+    out_copy.wait()
 
 
 def per_device(n_band, n_fft, band_coeffs, potential, stick_column, stick_length, orbitals):
@@ -361,12 +366,12 @@
     last = (n_band, per, cols)
     vm, sem = pltpu.VMEM, pltpu.SemaphoreType.DMA
     n_rows = count // LANES
-    return pl.pallas_call(
+    full, parts = pl.pallas_call(
         functools.partial(kernel, n_band, n_fft),
         out_shape=(
-            jax.ShapeDtypeStruct(band_coeffs.shape, BF), jax.ShapeDtypeStruct((per, cols), F32)),
+            jax.ShapeDtypeStruct(band_coeffs.shape, F32), jax.ShapeDtypeStruct((2, per, cols), F32)),
         in_specs=[pl.BlockSpec(memory_space=pl.ANY)] * 13,
-        out_specs=(pl.BlockSpec(memory_space=pltpu.VMEM),) * 2,
+        out_specs=(pl.BlockSpec(memory_space=pl.ANY), pl.BlockSpec(memory_space=pltpu.VMEM)),
         scratch_shapes=[
             vm(band_coeffs.shape, F32), vm(potential.shape, F32), vm((n_rows, LANES), I32),
             vm((1, sticks), I32), vm(orbitals.shape, BF)]
@@ -376,11 +381,22 @@
             vm((bands, 2 * planes, count), F32), vm((SUB * blocks, count), BF),
             vm((blocks, half, LANES), BF), vm((SUB * blocks, cells), BF)]
         + [vm(first, BF)] * 4 + [vm(swap, BF)] * 2 + [vm(fold, F32)] * 2 + [vm(last, F32)] * 2
-        + [sem((n_rows + 12,)), sem((3, n_fft)), sem((3, n_fft)), sem((2, n_band)), sem((2, n_band))],
+        + [vm(band_coeffs.shape, F32), sem(()), sem((n_rows + 12,)), sem((3, n_fft)), sem((3, n_fft)), sem((2, n_band)), sem((2, n_band))],
         compiler_params=pltpu.CompilerParams(
             collective_id=0, has_side_effects=True, vmem_limit_bytes=60 * 1024 * 1024),
         name="hamiltonian",
     )(band_coeffs, potential, stick_column, stick_length, orbitals, *[jnp.asarray(t) for t in tables])
+    def finish(full_ref, parts_ref, applied_ref, margin_ref):
+        applied_ref[...] = full_ref[...].astype(BF)
+        margin_ref[...] = parts_ref[0] + parts_ref[1]
+
+    return pl.pallas_call(
+        finish,
+        out_shape=(jax.ShapeDtypeStruct(band_coeffs.shape, BF), jax.ShapeDtypeStruct((per, cols), F32)),
+        in_specs=[pl.BlockSpec(memory_space=pltpu.VMEM)] * 2,
+        out_specs=(pl.BlockSpec(memory_space=pltpu.VMEM),) * 2,
+        name="finish",
+    )(full, parts)
 
 
 def solution(mesh):

time: 43.7 us -> 42.5 us (0.973)
  local copies, waits for them, and re-layouts: 2.72 us -> 0 us
  Pallas kernels: 40.2 us -> 41.7 us
    unnamed x2 -> x0, local copies, waits for them, and re-layouts: 2.72 us -> none
    pallas_call x0 -> x1, Pallas kernels: none -> 1.55 us  [per_device(): pl.pallas_call(finish, out_shape=(jax.ShapeDtypeStruct(band_coeffs.shape,...]
where the time goes in v4:
time: 42.5 us; the launch traced here: 42.4 us
  Pallas kernels  41.7 us (98%)
  between operations  0.64 us (2%)
    pallas_call x1, Pallas kernels, per_device(): pl.pallas_call(functools.partial(kernel, n_band, n_fft), out_shape=(jax.S...  40.2 us
    pallas_call x1, Pallas kernels, per_device(): pl.pallas_call(finish, out_shape=(jax.ShapeDtypeStruct(band_coeffs.shape,...  1.55 us

profile of v4, /device:TPU:1, one launch (start us, length us, event | category | flops | bytes accessed | tf_op | source)
XLA Modules:
  0.0 42.4 jit_solution(1453118602730152636)
XLA Ops:
  0.6 40.2 %hamiltonian.1 = (f32[2,64,192]{2,1,0:T(8,128)}, f32[2,4,32]{2,1,0:T(4,128)}) custom-call(f32[2,64,192]{2,1,0:T(8,128)} %coef_h.1, f32[12,192,192]{2,1,0:T(8,128)} %pot_h.1, s32[1024]{0:T(1024)} %col_h.1, s32[64]{0:T(128)} %len_h.1, bf16[8,192,512]{2,1,0:T(8,128)(2,1)} %bitcast.1, bf16[2,384,192]{2,1,0:T(8,128)(2,1)} %constant.16.clone.fz_h, ...), custom_call_target="tpu_custom_call" | custom-call | tf_op jit(solution)/shard_map/hamiltonian/pallas_call | solution.py:369
  40.8 1.5 %finish.1 = (bf16[2,64,192]{2,1,0:T(8,128)(2,1)}, f32[4,32]{1,0:T(4,128)}) custom-call(f32[2,64,192]{2,1,0:T(8,128)} %get-tuple-element.4.full_ref, f32[2,4,32]{2,1,0:T(4,128)} %get-tuple-element.5.parts_ref), custom_call_target="tpu_custom_call" | custom-call | tf_op jit(solution)/shard_map/finish/pallas_call | solution.py:393

commit v5 on v4

--- a/solution.py
+++ b/solution.py
@@ -81,12 +81,35 @@
     return jnp.concatenate(parts, axis=axis)
 
 
+DIGITS = {"fft": ((2, 1), (4, 1), (2, 0)), "band": ((2, 2), (4, 1))}
+
+
+def partners(axis, n):
+    digits = DIGITS[axis]
+    assert math.prod(size for size, _ in digits) == n
+    me = lax.axis_index(axis)
+    mine, offsets, stride = [], [()], n
+    for size, _ in digits:
+        stride //= size
+        mine.append((lax.rem(me // stride, size), size, stride))
+        offsets = [o + (k,) for o in offsets for k in range(size)]
+
+    def hops(offset):
+        return sum(min(k, size - k) * cost for k, (size, cost) in zip(offset, digits))
+
+    found = []
+    for k, offset in sorted(enumerate(offsets), key=lambda item: -hops(item[1])):
+        if k:
+            found.append((k, sum(
+                lax.rem(at + step, size) * stride for step, (at, size, stride) in zip(offset, mine))))
+    return found
+
+
 class Exchange:
     def __init__(self, axis, n, src, dst, send_sem, recv_sem):
         me = lax.axis_index(axis)
         self.copies = []
-        for k in range(1, n):
-            peer = lax.rem(me + k, n)
+        for k, peer in partners(axis, n):
             self.copies.append(pltpu.make_async_remote_copy(
                 src_ref=src.at[peer], dst_ref=dst.at[me],
                 send_sem=send_sem.at[k], recv_sem=recv_sem.at[k],
@@ -224,14 +247,12 @@
     coef, pot, q, length, orb, fz, fya, fyb, fx, fxb, ya, yb, fzb,
     w1, w1t, oxl, cfb, lhs, gbox, pk,
     send1, recv1, send2, recv2, send3, recv3, send4, recv4, send5, recv5,
-    kept_h, out_sem, load_sem, fft_send, fft_recv, band_send, band_recv,
+    load_sem, fft_send, fft_recv, band_send, band_recv,
 ):
     barrier = pltpu.get_barrier_semaphore()
     for axis, n in (("fft", n_fft), ("band", n_band)):
-        me = lax.axis_index(axis)
-        for k in range(1, n):
-            pl.semaphore_signal(
-                barrier, inc=1, device_id={axis: lax.rem(me + k, n)}, device_id_type=MESH)
+        for _, peer in partners(axis, n):
+            pl.semaphore_signal(barrier, inc=1, device_id={axis: peer}, device_id_type=MESH)
     loads = {}
     order = [
         (len_h, length.at[0])] + [
@@ -307,9 +328,7 @@
         tail = join([a[:, LANES:], b[:, LANES:]], 1)
         send3[r] = join([a[:, :LANES], b[:, :LANES], tail], 0).astype(BF)
     exchanges[2].start()
-    kept_h[...] = h.reshape(kept_h.shape)
-    out_copy = pltpu.make_async_copy(kept_h, applied, out_sem)
-    out_copy.start()
+    applied[...] = h.reshape(applied.shape)
     exchanges[2].wait()
 
     ours = recv3[...].astype(F32)
@@ -345,7 +364,6 @@
         for r in range(pair * part + 1, pair * (part + 1)):
             total = total + recv5[r]
         margin[part] = total
-    out_copy.wait()
 
 
 def per_device(n_band, n_fft, band_coeffs, potential, stick_column, stick_length, orbitals):
@@ -369,9 +387,9 @@
     full, parts = pl.pallas_call(
         functools.partial(kernel, n_band, n_fft),
         out_shape=(
-            jax.ShapeDtypeStruct(band_coeffs.shape, F32), jax.ShapeDtypeStruct((2, per, cols), F32)),
+            pltpu.VMEM(band_coeffs.shape, F32), pltpu.VMEM((2, per, cols), F32)),
         in_specs=[pl.BlockSpec(memory_space=pl.ANY)] * 13,
-        out_specs=(pl.BlockSpec(memory_space=pl.ANY), pl.BlockSpec(memory_space=pltpu.VMEM)),
+        out_specs=(pl.BlockSpec(memory_space=pltpu.VMEM),) * 2,
         scratch_shapes=[
             vm(band_coeffs.shape, F32), vm(potential.shape, F32), vm((n_rows, LANES), I32),
             vm((1, sticks), I32), vm(orbitals.shape, BF)]
@@ -381,9 +399,9 @@
             vm((bands, 2 * planes, count), F32), vm((SUB * blocks, count), BF),
             vm((blocks, half, LANES), BF), vm((SUB * blocks, cells), BF)]
         + [vm(first, BF)] * 4 + [vm(swap, BF)] * 2 + [vm(fold, F32)] * 2 + [vm(last, F32)] * 2
-        + [vm(band_coeffs.shape, F32), sem(()), sem((n_rows + 12,)), sem((3, n_fft)), sem((3, n_fft)), sem((2, n_band)), sem((2, n_band))],
+        + [sem((n_rows + 12,)), sem((3, n_fft)), sem((3, n_fft)), sem((2, n_band)), sem((2, n_band))],
         compiler_params=pltpu.CompilerParams(
-            collective_id=0, has_side_effects=True, vmem_limit_bytes=60 * 1024 * 1024),
+            collective_id=0, has_side_effects=True, vmem_limit_bytes=54 * 1024 * 1024),
         name="hamiltonian",
     )(band_coeffs, potential, stick_column, stick_length, orbitals, *[jnp.asarray(t) for t in tables])
     def finish(full_ref, parts_ref, applied_ref, margin_ref):
@@ -395,6 +413,7 @@
         out_shape=(jax.ShapeDtypeStruct(band_coeffs.shape, BF), jax.ShapeDtypeStruct((per, cols), F32)),
         in_specs=[pl.BlockSpec(memory_space=pltpu.VMEM)] * 2,
         out_specs=(pl.BlockSpec(memory_space=pltpu.VMEM),) * 2,
+        compiler_params=pltpu.CompilerParams(vmem_limit_bytes=4 * 1024 * 1024),
         name="finish",
     )(full, parts)
 

time: 42.5 us -> 40.3 us (0.948)
  Pallas kernels: 41.7 us -> 39.5 us
    pallas_call x1, Pallas kernels: 40.2 us -> 38.9 us  [per_device(): pl.pallas_call(functools.partial(kernel, n_band, n_fft), out_shape=(pltpu...]
    pallas_call x1, Pallas kernels: 1.55 us -> 0.64 us  [per_device(): pl.pallas_call(finish, out_shape=(jax.ShapeDtypeStruct(band_coeffs.shape,...]
where the time goes in v5:
time: 40.3 us; the launch traced here: 40.2 us
  Pallas kernels  39.5 us (98%)
  between operations  0.64 us (2%)
    pallas_call x1, Pallas kernels, per_device(): pl.pallas_call(functools.partial(kernel, n_band, n_fft), out_shape=(pltpu...  38.9 us

profile of v5, /device:TPU:1, one launch (start us, length us, event | category | flops | bytes accessed | tf_op | source)
XLA Modules:
  0.0 40.2 jit_solution(15323542139924042798)
XLA Ops:
  0.6 38.9 %hamiltonian.1 = (f32[2,64,192]{2,1,0:T(8,128)S(1)}, f32[2,4,32]{2,1,0:T(4,128)S(1)}) custom-call(f32[2,64,192]{2,1,0:T(8,128)} %coef_h.1, f32[12,192,192]{2,1,0:T(8,128)} %pot_h.1, s32[1024]{0:T(1024)} %col_h.1, s32[64]{0:T(128)} %len_h.1, bf16[8,192,512]{2,1,0:T(8,128)(2,1)} %bitcast.1, bf16[2,384,192]{2,1,0:T(8,128)(2,1)} %constant.16.clone.fz_h, ...), custom_call_target="tpu_custom_call" | custom-call | tf_op jit(solution)/shard_map/hamiltonian/pallas_call | solution.py:387
  39.5 0.6 %finish.1 = (bf16[2,64,192]{2,1,0:T(8,128)(2,1)}, f32[4,32]{1,0:T(4,128)}) custom-call(f32[2,64,192]{2,1,0:T(8,128)S(1)} %get-tuple-element.4.full_ref, f32[2,4,32]{2,1,0:T(4,128)S(1)} %get-tuple-element.5.parts_ref), custom_call_target="tpu_custom_call" | custom-call | tf_op jit(solution)/shard_map/finish/pallas_call | solution.py:411

commit v6 on v5

--- a/solution.py
+++ b/solution.py
@@ -85,6 +85,10 @@
 
 
 def partners(axis, n):
+    return [(k, peer) for k, _, peer in ranked(axis, n)]
+
+
+def ranked(axis, n):
     digits = DIGITS[axis]
     assert math.prod(size for size, _ in digits) == n
     me = lax.axis_index(axis)
@@ -100,9 +104,39 @@
     found = []
     for k, offset in sorted(enumerate(offsets), key=lambda item: -hops(item[1])):
         if k:
-            found.append((k, sum(
+            found.append((k, hops(offset), sum(
                 lax.rem(at + step, size) * stride for step, (at, size, stride) in zip(offset, mine))))
     return found
+
+
+class Spread:
+    def __init__(self, n_band, n_fft, src, dst, sems):
+        home = {axis: lax.axis_index(axis) for axis in ("band", "fft")}
+        me = home["band"] * n_fft + home["fft"]
+        rows = [(0, 0, home["band"])] + [(k, far, peer) for k, far, peer in ranked("band", n_band)]
+        cols = [(0, 0, home["fft"])] + [(k, far, peer) for k, far, peer in ranked("fft", n_fft)]
+        pairs = [(far_b + far_f, b, f) for kb, far_b, b in rows for kf, far_f, f in cols if kb or kf]
+        pairs.sort(key=lambda item: -item[0])
+        self.copies = [
+            pltpu.make_async_remote_copy(
+                src_ref=src.at[b * n_fft + f], dst_ref=dst.at[me], send_sem=sems.at[0], recv_sem=sems.at[1],
+                device_id={"band": b, "fft": f}, device_id_type=MESH)
+            for _, b, f in pairs]
+        self.own = pltpu.make_async_copy(src.at[me], dst.at[me], sems.at[2])
+        others = pl.ds(0, n_band * n_fft - 1)
+        self.all = pltpu.make_async_remote_copy(
+            src_ref=src.at[others], dst_ref=dst.at[others], send_sem=sems.at[0], recv_sem=sems.at[1],
+            device_id=home, device_id_type=MESH)
+
+    def start(self):
+        for copy in self.copies:
+            copy.start()
+        self.own.start()
+
+    def wait(self):
+        self.own.wait()
+        self.all.wait_send()
+        self.all.wait_recv()
 
 
 class Exchange:
@@ -246,8 +280,8 @@
     applied, margin,
     coef, pot, q, length, orb, fz, fya, fyb, fx, fxb, ya, yb, fzb,
     w1, w1t, oxl, cfb, lhs, gbox, pk,
-    send1, recv1, send2, recv2, send3, recv3, send4, recv4, send5, recv5,
-    load_sem, fft_send, fft_recv, band_send, band_recv,
+    send1, recv1, send2, recv2, send3, recv3, send4, recv4,
+    load_sem, fft_send, fft_recv, band_send, band_recv, all_sem,
 ):
     barrier = pltpu.get_barrier_semaphore()
     for axis, n in (("fft", n_fft), ("band", n_band)):
@@ -268,8 +302,7 @@
         Exchange("fft", n_fft, send1, recv1, fft_send.at[0], fft_recv.at[0]),
         Exchange("fft", n_fft, send2, recv2, fft_send.at[1], fft_recv.at[1]),
         Exchange("band", n_band, send3, recv3, band_send.at[0], band_recv.at[0]),
-        Exchange("fft", n_fft, send4, recv4, fft_send.at[2], fft_recv.at[2]),
-        Exchange("band", n_band, send5, recv5, band_send.at[1], band_recv.at[1]),
+        Spread(n_band, n_fft, send4.reshape(n_band * n_fft, *send4.shape[2:]), recv4.reshape(n_band * n_fft, *send4.shape[2:]), all_sem),
     ]
 
     bands, sticks, width = coef.shape
@@ -309,7 +342,7 @@
 
     spread_sticks(recv1, oxl, cfb, lhs)
     place(lhs, w1, gbox)
-    count = 4
+    count = 6
     for first in range(0, pot.shape[0], count):
         apply_potential(first, count, gbox, pot, fya, fyb, fx, fxb, ya, yb, pk)
     pick(pk, w1t, oxl, lhs, send2)
@@ -343,27 +376,14 @@
         term = dot(both[:, j, :].astype(BF), orb[j])
         total = term if total is None else total + term
     total = total.T
-    per = total.shape[0] // (n_band * n_fft)
-    total = total.reshape(n_band, n_fft * per, total.shape[1])
-    total = join([total[r] for r in range(n_band)], 1)
-    for f in range(n_fft):
-        send4[f] = total[per * f : per * (f + 1)]
+    per = margin.shape[1]
+    total = total.reshape(n_band * n_fft // 2, 2 * per, total.shape[1])
+    for part in range(2):
+        send4[:, part] = total[:, per * part : per * (part + 1)]
     exchanges[3].start()
     exchanges[3].wait()
-    total = recv4[0]
-    for f in range(1, n_fft):
-        total = total + recv4[f]
-    cols = margin.shape[2]
-    for r in range(n_band):
-        send5[r] = total[:, cols * r : cols * (r + 1)]
-    exchanges[4].start()
-    exchanges[4].wait()
-    pair = n_band // 2
     for part in range(2):
-        total = recv5[pair * part]
-        for r in range(pair * part + 1, pair * (part + 1)):
-            total = total + recv5[r]
-        margin[part] = total
+        margin[part] = jnp.sum(recv4[:, part], axis=0)
 
 
 def per_device(n_band, n_fft, band_coeffs, potential, stick_column, stick_length, orbitals):
@@ -380,8 +400,7 @@
     first = (n_fft, 2 * planes, bands * sticks)
     swap = (n_band, bands * group * width // LANES, LANES)
     cols = 2 * n_band * bands
-    fold = (n_fft, per, n_band * cols)
-    last = (n_band, per, cols)
+    share = (n_band * n_fft // 2, 2, per, cols)
     vm, sem = pltpu.VMEM, pltpu.SemaphoreType.DMA
     n_rows = count // LANES
     full, parts = pl.pallas_call(
@@ -398,8 +417,8 @@
             vm((count, cells), BF), vm((cells, count), BF), vm((SUB, count), F32),
             vm((bands, 2 * planes, count), F32), vm((SUB * blocks, count), BF),
             vm((blocks, half, LANES), BF), vm((SUB * blocks, cells), BF)]
-        + [vm(first, BF)] * 4 + [vm(swap, BF)] * 2 + [vm(fold, F32)] * 2 + [vm(last, F32)] * 2
-        + [sem((n_rows + 12,)), sem((3, n_fft)), sem((3, n_fft)), sem((2, n_band)), sem((2, n_band))],
+        + [vm(first, BF)] * 4 + [vm(swap, BF)] * 2 + [vm(share, F32)] * 2
+        + [sem((n_rows + 12,)), sem((2, n_fft)), sem((2, n_fft)), sem((1, n_band)), sem((1, n_band)), sem((3,))],
         compiler_params=pltpu.CompilerParams(
             collective_id=0, has_side_effects=True, vmem_limit_bytes=54 * 1024 * 1024),
         name="hamiltonian",

time: 40.3 us -> 37.9 us (0.940)
  Pallas kernels: 39.5 us -> 37.1 us
    pallas_call x1, Pallas kernels: 38.9 us -> 36.5 us  [per_device(): pl.pallas_call(functools.partial(kernel, n_band, n_fft), out_shape=(pltpu...]
where the time goes in v6:
time: 37.9 us; the launch traced here: 37.8 us
  Pallas kernels  37.1 us (98%)
  between operations  0.64 us (2%)
    pallas_call x1, Pallas kernels, per_device(): pl.pallas_call(functools.partial(kernel, n_band, n_fft), out_shape=(pltpu...  36.5 us

profile of v6, /device:TPU:1, one launch (start us, length us, event | category | flops | bytes accessed | tf_op | source)
XLA Modules:
  0.0 37.8 jit_solution(5651122642632283045)
XLA Ops:
  0.6 36.5 %hamiltonian.1 = (f32[2,64,192]{2,1,0:T(8,128)S(1)}, f32[2,4,32]{2,1,0:T(4,128)S(1)}) custom-call(f32[2,64,192]{2,1,0:T(8,128)} %coef_h.1, f32[12,192,192]{2,1,0:T(8,128)} %pot_h.1, s32[1024]{0:T(1024)} %col_h.1, s32[64]{0:T(128)} %len_h.1, bf16[8,192,512]{2,1,0:T(8,128)(2,1)} %bitcast.1, bf16[2,384,192]{2,1,0:T(8,128)(2,1)} %constant.16.clone.fz_h, ...), custom_call_target="tpu_custom_call" | custom-call | tf_op jit(solution)/shard_map/hamiltonian/pallas_call | solution.py:406
  37.1 0.6 %finish.1 = (bf16[2,64,192]{2,1,0:T(8,128)(2,1)}, f32[4,32]{1,0:T(4,128)}) custom-call(f32[2,64,192]{2,1,0:T(8,128)S(1)} %get-tuple-element.4.full_ref, f32[2,4,32]{2,1,0:T(4,128)S(1)} %get-tuple-element.5.parts_ref), custom_call_target="tpu_custom_call" | custom-call | tf_op jit(solution)/shard_map/finish/pallas_call | solution.py:430

commit v7 on v6

--- a/solution.py
+++ b/solution.py
@@ -280,7 +280,7 @@
     applied, margin,
     coef, pot, q, length, orb, fz, fya, fyb, fx, fxb, ya, yb, fzb,
     w1, w1t, oxl, cfb, lhs, gbox, pk,
-    send1, recv1, send2, recv2, send3, recv3, send4, recv4,
+    send1, recv1, send2, recv2, send3, recv3, send4, recv4, sums,
     load_sem, fft_send, fft_recv, band_send, band_recv, all_sem,
 ):
     barrier = pltpu.get_barrier_semaphore()
@@ -302,7 +302,7 @@
         Exchange("fft", n_fft, send1, recv1, fft_send.at[0], fft_recv.at[0]),
         Exchange("fft", n_fft, send2, recv2, fft_send.at[1], fft_recv.at[1]),
         Exchange("band", n_band, send3, recv3, band_send.at[0], band_recv.at[0]),
-        Spread(n_band, n_fft, send4.reshape(n_band * n_fft, *send4.shape[2:]), recv4.reshape(n_band * n_fft, *send4.shape[2:]), all_sem),
+        Spread(n_band, n_fft, send4, recv4, all_sem),
     ]
 
     bands, sticks, width = coef.shape
@@ -376,14 +376,15 @@
         term = dot(both[:, j, :].astype(BF), orb[j])
         total = term if total is None else total + term
     total = total.T
-    per = margin.shape[1]
-    total = total.reshape(n_band * n_fft // 2, 2 * per, total.shape[1])
-    for part in range(2):
-        send4[:, part] = total[:, per * part : per * (part + 1)]
+    per = total.shape[0] // (n_band * n_fft)
+    everyone = send4.shape[0]
+    sums[...] = total
+    total = join([sums[pl.ds(i, everyone, stride=per), :] for i in range(per)], 1)
+    send4[...] = total.reshape(send4.shape)
     exchanges[3].start()
     exchanges[3].wait()
     for part in range(2):
-        margin[part] = jnp.sum(recv4[:, part], axis=0)
+        margin[part] = jnp.sum(recv4[everyone // 2 * part : everyone // 2 * (part + 1)], axis=0)
 
 
 def per_device(n_band, n_fft, band_coeffs, potential, stick_column, stick_length, orbitals):
@@ -400,13 +401,13 @@
     first = (n_fft, 2 * planes, bands * sticks)
     swap = (n_band, bands * group * width // LANES, LANES)
     cols = 2 * n_band * bands
-    share = (n_band * n_fft // 2, 2, per, cols)
+    share = (n_band * n_fft, 1, per * cols)
     vm, sem = pltpu.VMEM, pltpu.SemaphoreType.DMA
     n_rows = count // LANES
     full, parts = pl.pallas_call(
         functools.partial(kernel, n_band, n_fft),
         out_shape=(
-            pltpu.VMEM(band_coeffs.shape, F32), pltpu.VMEM((2, per, cols), F32)),
+            pltpu.VMEM(band_coeffs.shape, F32), pltpu.VMEM((2, 1, per * cols), F32)),
         in_specs=[pl.BlockSpec(memory_space=pl.ANY)] * 13,
         out_specs=(pl.BlockSpec(memory_space=pltpu.VMEM),) * 2,
         scratch_shapes=[
@@ -417,7 +418,7 @@
             vm((count, cells), BF), vm((cells, count), BF), vm((SUB, count), F32),
             vm((bands, 2 * planes, count), F32), vm((SUB * blocks, count), BF),
             vm((blocks, half, LANES), BF), vm((SUB * blocks, cells), BF)]
-        + [vm(first, BF)] * 4 + [vm(swap, BF)] * 2 + [vm(share, F32)] * 2
+        + [vm(first, BF)] * 4 + [vm(swap, BF)] * 2 + [vm(share, F32)] * 2 + [vm((rows, cols), F32)]
         + [sem((n_rows + 12,)), sem((2, n_fft)), sem((2, n_fft)), sem((1, n_band)), sem((1, n_band)), sem((3,))],
         compiler_params=pltpu.CompilerParams(
             collective_id=0, has_side_effects=True, vmem_limit_bytes=54 * 1024 * 1024),
@@ -425,7 +426,8 @@
     )(band_coeffs, potential, stick_column, stick_length, orbitals, *[jnp.asarray(t) for t in tables])
     def finish(full_ref, parts_ref, applied_ref, margin_ref):
         applied_ref[...] = full_ref[...].astype(BF)
-        margin_ref[...] = parts_ref[0] + parts_ref[1]
+        both = parts_ref[0] + parts_ref[1]
+        margin_ref[...] = join([both[:, cols * i : cols * (i + 1)] for i in range(per)], 0)
 
     return pl.pallas_call(
         finish,

time: 37.9 us -> 37.4 us (0.987)
  Pallas kernels: 37.1 us -> 36.7 us
    pallas_call x1, Pallas kernels: 36.5 us -> 36 us  [per_device(): pl.pallas_call(functools.partial(kernel, n_band, n_fft), out_shape=(pltpu...]
where the time goes in v7:
time: 37.4 us; the launch traced here: 37.3 us
  Pallas kernels  36.7 us (98%)
  between operations  0.64 us (2%)
    pallas_call x1, Pallas kernels, per_device(): pl.pallas_call(functools.partial(kernel, n_band, n_fft), out_shape=(pltpu...  36 us

profile of v7, /device:TPU:1, one launch (start us, length us, event | category | flops | bytes accessed | tf_op | source)
XLA Modules:
  0.0 37.3 jit_solution(17231510783704601855)
XLA Ops:
  0.6 36.0 %hamiltonian.1 = (f32[2,64,192]{2,1,0:T(8,128)S(1)}, f32[2,1,128]{2,1,0:T(1,128)S(1)}) custom-call(f32[2,64,192]{2,1,0:T(8,128)} %coef_h.1, f32[12,192,192]{2,1,0:T(8,128)} %pot_h.1, s32[1024]{0:T(1024)} %col_h.1, s32[64]{0:T(128)} %len_h.1, bf16[8,192,512]{2,1,0:T(8,128)(2,1)} %bitcast.1, bf16[2,384,192]{2,1,0:T(8,128)(2,1)} %constant.16.clone.fz_h, ...), custom_call_target="tpu_custom_call" | custom-call | tf_op jit(solution)/shard_map/hamiltonian/pallas_call | solution.py:407
  36.7 0.7 %finish.1 = (bf16[2,64,192]{2,1,0:T(8,128)(2,1)}, f32[4,32]{1,0:T(4,128)}) custom-call(f32[2,64,192]{2,1,0:T(8,128)S(1)} %get-tuple-element.4.full_ref, f32[2,1,128]{2,1,0:T(1,128)S(1)} %get-tuple-element.5.parts_ref), custom_call_target="tpu_custom_call" | custom-call | tf_op jit(solution)/shard_map/finish/pallas_call | solution.py:432
